TPU v7x, 512 devices: a whole 4x8x8 slice. The times are simulated.
512 devices in a mesh: ctx: 16 (over z, core), ch: 32 (over x, y).
Axes of the slice: x: 4, y: 8, z: 8, core: 2. Of those that a mesh axis runs over, the one named last changes fastest.
Arguments:
- features: bfloat16 [3, 4096, 8192], P(None, 'ctx', 'ch'), may hold values from -6 to 6
- short_weight: float32 [3, 7, 8192], P(None, None, 'ch'), may hold values from -2 to 2
- rates: float32 [8192, 16], P('ch'), may hold values from 7.324219e-05 to 0.08
- residues: float32 [8192, 16], P('ch'), may hold values from -0.75 to 0.75
- skip: float32 [8192], P('ch'), may hold values from -4 to 4
- out_weight: bfloat16 [8192, 8192], P('ctx', 'ch'), may hold values from -0.0625 to 0.0625
Outputs:
- mixed: bfloat16 [4096, 8192], P('ctx', 'ch')
All inputs are finite; a program needn't handle non-finite values.
Results may differ from a plain program's by a relative error of at most 0.0076.
Values may be sent and summed in bfloat16 or wider, within the bound.
No kernel may reach another device: no remote copies, remote signals or barrier semaphores. Data moves between devices by JAX's collectives and lax.ppermute only.
A program may use at most 64 MiB of HBM per device.

v0:
```python
import jax
import jax.numpy as jnp
from jax import lax
from jax.sharding import PartitionSpec as P

STRETCH = 64


def passed_along(value, axis, by):
    length = lax.axis_size(axis)
    pairs = [(i, i + by) for i in range(length) if 0 <= i + by < length]
    return lax.ppermute(value, axis, pairs)


def prefix_2(value, axis, combine, identity):
    length, place = (lax.axis_size(axis), lax.axis_index(axis))
    everything = jax.tree.map(lambda part: lax.all_gather(part, axis), value)
    start = jax.tree.map(
        lambda part, zero: jnp.broadcast_to(jnp.asarray(zero, part.dtype), part.shape),
        value,
        identity,
    )

    def lap(k, before):
        reached = k < place
        new = combine(before, jax.tree.map(lambda part: part[k], everything))
        return jax.tree.map(lambda a, b: jnp.where(reached, a, b), new, before)

    return lax.fori_loop(0, length, lap, start)


def join_states(earlier, later):
    return (earlier[0] * later[0], earlier[1] * later[0] + later[1])


def per_device(features, short_weight, rates, residues, skip, out_weight):
    kernel_width = short_weight.shape[1]
    local_rows = features.shape[1]
    local_chans = features.shape[2]
    highest = lax.Precision.HIGHEST
    left_rim = passed_along(features[:, local_rows - (kernel_width - 1) :, :], "ctx", 1)
    extended = jnp.concatenate([left_rim, features], axis=1).astype(jnp.float32)
    featured = jnp.zeros((3, local_rows, local_chans), jnp.float32)
    for offset in range(kernel_width):
        featured = (
            featured
            + short_weight[:, offset][:, None, :]
            * extended[:, kernel_width - 1 - offset : kernel_width - 1 - offset + local_rows, :]
        )
    featured = featured.astype(jnp.bfloat16)
    query = featured[0].astype(jnp.float32)
    product = (featured[1].astype(jnp.float32) * featured[2].astype(jnp.float32)).astype(
        jnp.bfloat16
    )
    product_value = product.astype(jnp.float32)
    block_count = local_rows // STRETCH
    decay_rate = rates.T
    mode_gain = residues.T
    block_lag = jnp.arange(STRETCH, dtype=jnp.float32)
    block_index = jnp.arange(STRETCH, dtype=jnp.int32)
    short_filter = jnp.einsum(
        "nc,nca->ca",
        mode_gain,
        jnp.exp(-decay_rate[:, :, None] * block_lag[None, None, :]),
        precision=highest,
    )
    lag_table = block_index[:, None] - block_index[None, :]
    toeplitz = jnp.where(
        (lag_table >= 0)[None, :, :], short_filter[:, jnp.maximum(lag_table, 0)], 0.0
    )
    blocks = product_value.reshape(block_count, STRETCH, local_chans)
    inner_part = jnp.einsum("cab,kbc->kac", toeplitz, blocks, precision=highest)
    to_block_end = jnp.exp(-decay_rate[None, :, :] * (STRETCH - 1 - block_lag)[:, None, None])
    block_states = jnp.einsum("kbc,bnc->knc", blocks, to_block_end, precision=highest)
    block_decay = jnp.exp(-decay_rate * STRETCH)

    def advance(state_now, block_state):
        return (block_decay * state_now + block_state, state_now)

    local_total, states_before = lax.scan(advance, jnp.zeros_like(decay_rate), block_states)
    span_decay = jnp.exp(-decay_rate * local_rows)
    prefix = prefix_2(
        (span_decay, local_total),
        "ctx",
        join_states,
        (jnp.ones_like(decay_rate), jnp.zeros_like(decay_rate)),
    )
    incoming = prefix[1]
    block_offset = jnp.arange(block_count, dtype=jnp.float32) * STRETCH
    start_states = (
        jnp.exp(-decay_rate[None, :, :] * block_offset[:, None, None]) * incoming[None, :, :]
        + states_before
    )
    mode_output = mode_gain[None, :, :] * jnp.exp(
        -decay_rate[None, :, :] * (block_lag + 1.0)[:, None, None]
    )
    outer_part = jnp.einsum("knc,anc->kac", start_states, mode_output, precision=highest)
    conv_value = (inner_part + outer_part).reshape(local_rows, local_chans) + skip[
        None, :
    ] * product_value
    gated = (query * conv_value).astype(jnp.bfloat16)
    whole_rows = lax.all_gather(gated, "ch", axis=1, tiled=True)
    mixed = jnp.dot(
        whole_rows,
        lax.all_gather(out_weight, "ctx", axis=0, tiled=True),
        preferred_element_type=jnp.float32,
    )
    return mixed.astype(jnp.bfloat16)


def solution(mesh):
    return jax.shard_map(
        per_device,
        mesh=mesh,
        in_specs=(
            P(None, "ctx", "ch"),
            P(None, None, "ch"),
            P("ch", None),
            P("ch", None),
            P("ch"),
            P("ctx", "ch"),
        ),
        out_specs=P("ctx", "ch"),
        check_vma=False,
    )
```

profile of v0, /device:TPU:4, one launch (start us, length us, event | category | flops | bytes accessed | tf_op | source)
XLA Modules:
  0.0 195.4 jit_solution(18356100601108035433)
XLA Ops:
  6.5 0.0 all-gather.7.cloned.1.call-start
  6.5 0.7 slice.55
  7.2 1.7 collective-permute-start
  9.0 0.0 all-gather.7.cloned.1.call-update
  9.0 0.0 all-gather.5.cloned.1.call-start
  9.1 0.7 negate_bitcast_fusion
  9.8 0.7 multiply_exponential_fusion.1
  10.6 1.1 fusion.41
  11.6 0.1 reshape.74
  11.7 24.6 %all-gather = f32[256,256]{1,0:T(8,128)S(1)} all-gather(f32[16,256]{1,0:T(8,128)S(1)} %get-tuple-element.203), channel_id=2, replica_groups=mesh['ctx'=16,'ch'=32] {'ctx'}, dimensions={0}, use_global_device_ids=true | all-gather | bytes 278528 | tf_op jit(solution)/shard_map/all_gather | solution.py:17
  36.3 1.9 multiply_reduce_fusion
  38.3 0.1 copy.18
  38.4 0.1 copy.29
  38.5 16.2 %gather_fusion = f32[4096,256]{1,0:T(8,128)} fusion(f32[256,64]{0,1:T(8,128)S(1)} %copy.29, s32[4096]{0:T(1024)S(1)} %broadcast_clamp_fusion), kind=kCustom, calls=%fused_computation | custom fusion | bytes 8404992 | tf_op jit(solution)/shard_map/gather | solution.py:69
  54.7 0.0 copy-start.1
  54.7 0.0 copy-start
  54.7 9.2 %copy.15 = f32[64,64,256]{1,0,2:T(8,128)} copy(f32[64,64,256]{2,1,0:T(8,128)} %bitcast.80) | data formatting | bytes 8388608 | tf_op jit(solution)/shard_map/gather | solution.py:69
  63.9 0.0 copy-done.1
  63.9 0.1 copy.17
  64.0 0.0 collective-permute-done
  64.0 0.0 copy-done
  64.0 0.1 maximum_convert_fusion
  64.1 0.7 fusion.31
  64.8 0.2 copy.16
  65.0 2.0 %fusion.19 = f32[4,16,256]{1,0,2:T(4,128)S(1)} fusion(bf16[4,64,256]{1,0,2:T(4,128)(2,1)S(1)} %copy.16, f32[64]{0:T(128)S(1)} %iota_subtract_fusion, f32[16,256]{0,1:T(8,128)S(1)} %copy.18), kind=kOutput, calls=%fused_computation.21 | convolution fusion | flops 12845056 | bytes 213248 | tf_op jit(solution)/shard_map/kbc,bnc->knc/dot_general | solution.py:74
  67.0 0.2 copy.20
  67.2 0.2 while.27
  67.4 15.2 %all-gather.1 = f32[256,256]{1,0:T(8,128)S(1)} all-gather(f32[16,256]{1,0:T(8,128)S(1)} %get-tuple-element.127), channel_id=3, replica_groups=mesh['ctx'=16,'ch'=32] {'ctx'}, dimensions={0}, use_global_device_ids=true | all-gather | bytes 278528 | tf_op jit(solution)/shard_map/all_gather | solution.py:17
  82.6 0.6 while.28
  83.2 0.1 multiply_add_fusion
  83.3 0.2 copy.21
  83.5 8.9 %fusion.22 = f32[4,64,256]{1,0,2:T(4,128)S(1)} fusion(bf16[4,64,256]{1,0,2:T(4,128)(2,1)S(1)} %copy.16, f32[64,64,256]{1,0,2:T(8,128)} %copy.15, pred[64,64]{1,0:T(8,128)(4,1)S(1)} %subtract_compare_fusion), kind=kOutput, calls=%fused_computation.22 | convolution fusion | flops 51380224 | bytes 4591616 | tf_op jit(solution)/shard_map/cab,kbc->kac/dot_general | solution.py:72
  92.4 0.0 copy-start.2
  92.4 3.1 %fusion.16 = f32[4,64,256]{1,0,2:T(4,128)S(1)} fusion(f32[4,64,256]{1,0,2:T(4,128)S(1)} %fusion.22, f32[4,16,256]{1,0,2:T(4,128)S(1)} %copy.21, f32[64]{0:T(128)S(1)} %iota_add_fusion, f32[16,256]{0,1:T(8,128)S(1)} %copy.18, f32[16,256]{0,1:T(8,128)S(1)} %copy.17), kind=kOutput, calls=%fused_computation.20 | convolution fusion | flops 13172736 | bytes 622848 | tf_op jit(solution)/shard_map/knc,anc->kac/dot_general | solution.py:97
  95.6 0.2 copy.22
  95.8 0.0 copy-done.2
  95.8 0.7 fusion.39
  96.5 0.0 all-gather.5.cloned.1.call-update
  96.5 0.0 all-gather.7.cloned.1.call-done
  96.6 86.7 %all-gather.5.cloned.1.call-done = bf16[256,8192]{1,0:T(8,128)(2,1)} async-done(((bf16[256,256]{1,0:T(8,128)(2,1)}), bf16[256,8192]{1,0:T(8,128)(2,1)}) %all-gather.5.cloned.1.call-update) | async-done | bytes 4194320 | tf_op jit(solution)/shard_map/all_gather | solution.py:102
  183.2 5.4 %convolution_convert_fusion = bf16[256,256]{1,0:T(8,128)(2,1)} fusion(bf16[256,8192]{1,0:T(8,128)(2,1)} %all-gather.5.cloned.1.call-done, bf16[8192,256]{1,0:T(8,128)(2,1)} %all-gather.7.cloned.1.call-done), kind=kOutput, calls=%fused_computation.23 | convolution fusion | flops 1073807360 | bytes 8519680 | tf_op jit(solution)/shard_map/dot_general | solution.py:103
  (38 shorter events, 0.4 us)
Async XLA Ops:
  6.5 90.0 %all-gather.7.cloned.1.call-start = ((), (), s32[]{:S(2)}) async-start(), calls=%async_computation.1 | async-start | bytes 4456448 | tf_op jit(solution)/shard_map/all_gather | solution.py:105
  7.2 56.8 %collective-permute-start = (bf16[3,6,256]{2,1,0:T(8,128)(2,1)S(1)}, bf16[3,6,256]{2,1,0:T(8,128)(2,1)S(1)}, u32[]{:S(2)}, u32[]{:S(2)}) collective-permute-start(bf16[3,6,256]{2,1,0:T(8,128)(2,1)S(1)} %slice.55), channel_id=1, source_target_pairs={{0,32},{32,64},{64,96},{96,128},{128,160},{160,192},{192,224},{224... | collective-permute-start | bytes 27656 | tf_op jit(solution)/shard_map/ppermute | solution.py:12
  9.0 174.2 %all-gather.5.cloned.1.call-start = ((), (), s32[]{:S(2)}) async-start(), calls=%async_computation | async-start | bytes 4325376 | tf_op jit(solution)/shard_map/all_gather | solution.py:102
  54.7 9.2 %copy-start.1 = (f32[256,16]{0,1:T(8,128)S(1)}, f32[256,16]{0,1:T(8,128)}, u32[]{:S(2)}) copy-start(f32[256,16]{0,1:T(8,128)} %param.13) | copy-start | bytes 49156
  54.7 9.3 %copy-start = (bf16[3,256,256]{2,1,0:T(8,128)(2,1)S(1)}, bf16[3,256,256]{2,1,0:T(8,128)(2,1)}, u32[]{:S(2)}) copy-start(bf16[3,256,256]{2,1,0:T(8,128)(2,1)} %param.10) | copy-start | bytes 1179652
  92.4 3.3 %copy-start.2 = (f32[256]{0:T(256)S(1)}, f32[256]{0:T(256)}, u32[]{:S(2)}) copy-start(f32[256]{0:T(256)} %param.14) | copy-start | bytes 3076
Sparse Core Ops, SparseCore 0:
  9.4 50.9 all-gather.6
  96.6 86.5 all-gather.4
where the time goes:
time: 196 us; the launch traced here: 195 us
  waiting for transfers between devices  86.7 us (44%)
  blocking collectives  39.8 us (20%)
  local copies, waits for them, and re-layouts  28.3 us (14%)
  matrix products  19.4 us (10%)
  between operations  13.6 us (7%)
  other arithmetic  5.3 us (3%)
    all_gather x1, waiting for transfers between devices, per_device(): whole_rows = lax.all_gather(gated, 'ch', axis=1, tiled=True)  86.7 us
    all_gather x2, blocking collectives, prefix_2(): everything = jax.tree.map(lambda part: lax.all_gather(part, axis), value)  39.8 us
    gather x2, local copies, waits for them, and re-layouts, per_device(): short_filter[:, jnp.maximum(lag_table, 0)]  25.4 us
    dot_general x1, matrix products, per_device(): inner_part = jnp.einsum('cab,kbc->kac', toeplitz, blocks, precision=highest)  8.93 us
    dot_general x1, matrix products, per_device(): jnp.dot(whole_rows, lax.all_gather(out_weight, 'ctx', axis=0, tiled=True)...  5.37 us
  transfers between devices with their start and end apart: 3, of which 1 were waited for; matrix products, arithmetic and copies ran while one was open for 24% of the time, Pallas kernels for 0%

commit v1 on v0

v1 whole, which is shorter than its diff:
```python
import functools

import jax
import jax.numpy as jnp
from jax import lax
from jax.experimental import pallas as pl
from jax.experimental.pallas import tpu as pltpu
from jax.sharding import Mesh
from jax.sharding import PartitionSpec as P

STRETCH = 64
RIM = 8
SHAPE = {"c": 2, "x": 4}
F32 = jnp.float32
BF16 = jnp.bfloat16
CTX = ("z", "c")
CH = ("x", "y")
VMEM = pl.BlockSpec(memory_space=pltpu.VMEM)
SMEM = pl.BlockSpec(memory_space=pltpu.SMEM)


def local_kernel(features, rim, taps, rates, gains, skip, query, inner, before, totals, extended, product):
    streams, rows, chans = features.shape
    width = taps.shape[1]
    modes = rates.shape[0]
    stretches = rows // STRETCH
    piece = 32
    for f in range(streams):
        extended[f, 0:RIM, :] = rim[f].astype(F32)
        extended[f, RIM : RIM + rows, :] = features[f].astype(F32)
    for start in range(0, rows, piece):
        parts = []
        for f in range(streams):
            total = jnp.zeros((piece, chans), F32)
            for offset in range(width):
                at = RIM + start - offset
                total = total + taps[f, offset : offset + 1, :] * extended[f, at : at + piece, :]
            parts.append(total.astype(BF16))
        query[start : start + piece, :] = parts[0]
        product[start : start + piece, :] = (
            (parts[1].astype(F32) * parts[2].astype(F32)).astype(BF16).astype(F32)
        )
    decay = jnp.exp(-rates[...])
    gain = gains[...]
    through = skip[...]

    def eight(i, states):
        states = list(states)
        base = pl.multiple_of(i * 8, 8)
        for k in range(stretches):
            at = pl.multiple_of(k * STRETCH + base, 8)
            tile = product[pl.ds(at, 8), :]
            outs = []
            state = states[k]
            for r in range(8):
                state = decay * state + jnp.broadcast_to(tile[r : r + 1, :], (modes, chans))
                outs.append(jnp.sum(gain * state, axis=0, keepdims=True))
            states[k] = state
            inner[pl.ds(at, 8), :] = jnp.concatenate(outs, axis=0) + through * tile
        return tuple(states)

    zero = jnp.zeros((modes, chans), F32)
    states = lax.fori_loop(0, STRETCH // 8, eight, (zero,) * stretches)
    across = jnp.exp(-rates[...] * STRETCH)
    running = zero
    for k in range(stretches):
        before[k] = running
        running = across * running + states[k]
    for i in range(totals.shape[0]):
        totals[i] = running


def join_kernel(place, everyone, before, inner, query, table, rates, out, starts, gated):
    length, modes, chans = everyone.shape
    stretches = before.shape[0]
    rows = inner.shape[0]
    me = place[0]
    span = jnp.exp(-rates[...] * rows)
    incoming = jnp.zeros((modes, chans), F32)
    for i in range(length):
        incoming = jnp.where(i < me, span * incoming + everyone[i], incoming)
    for k in range(stretches):
        starts[k] = jnp.exp(-rates[...] * (k * STRETCH)) * incoming + before[k]

    def eight(i, carry):
        base = pl.multiple_of(i * 8, 8)
        totals = [inner[pl.ds(pl.multiple_of(k * STRETCH + base, 8), 8), :] for k in range(stretches)]
        for n in range(modes):
            weight = table[n, pl.ds(base, 8), :]
            for k in range(stretches):
                totals[k] = totals[k] + weight * starts[k, n : n + 1, :]
        for k in range(stretches):
            at = pl.multiple_of(k * STRETCH + base, 8)
            gated[pl.ds(at, 8), :] = query[pl.ds(at, 8), :].astype(F32) * totals[k]
        return carry

    lax.fori_loop(0, STRETCH // 8, eight, 0)
    turned = gated[...].T.astype(BF16)
    blocks = out.shape[0]
    height = out.shape[2]
    for b in range(blocks):
        for copy in range(out.shape[1]):
            out[b, copy] = turned[b * height : (b + 1) * height, :]


def project_kernel(gated, weight, out):
    depth = gated.shape[0] * gated.shape[1]
    left = gated[...].reshape(depth, gated.shape[2])
    right = weight[...].reshape(depth, weight.shape[3])
    out[0] = lax.dot_general(left, right, (((0,), (0,)), ((), ())), preferred_element_type=F32).astype(BF16)


def call(kernel, out_shape, scratch, flops, moved, in_specs, name):
    return pl.pallas_call(
        kernel,
        out_shape=out_shape,
        in_specs=in_specs,
        out_specs=jax.tree.map(lambda _: VMEM, out_shape),
        scratch_shapes=scratch,
        cost_estimate=pl.CostEstimate(flops=flops, bytes_accessed=moved, transcendentals=0),
        compiler_params=pltpu.CompilerParams(vmem_limit_bytes=32 << 20),
        name=name,
    )


def per_device(features, short_weight, rates, residues, skip, out_weight):
    streams, rows, chans = features.shape
    modes = rates.shape[1]
    length = lax.axis_size(CTX)
    xs, ys = lax.axis_size("x"), lax.axis_size("y")
    place = lax.axis_index(CTX)
    decay_rate = rates.T
    mode_gain = residues.T
    shape = jax.ShapeDtypeStruct

    rim = lax.ppermute(features[:, rows - RIM :, :], CTX, [(i, i + 1) for i in range(length - 1)])

    deep, wide = out_weight.shape
    owned = deep // chans
    piece = chans // xs
    sliced = out_weight.reshape(owned, xs, piece, wide).transpose(1, 0, 2, 3).reshape(xs, owned * piece, wide)
    sliced = lax.all_to_all(sliced, "x", split_axis=0, concat_axis=0, tiled=True)
    weights = lax.all_gather(sliced, CTX, axis=0, tiled=False)

    lag = jnp.arange(STRETCH, dtype=F32) + 1.0
    table = mode_gain[:, None, :] * jnp.exp(-decay_rate[:, None, :] * lag[None, :, None])
    rim, sliced, table = lax.optimization_barrier((rim, sliced, table))

    stretches = rows // STRETCH
    query, inner, before, totals = call(
        local_kernel,
        (
            shape((rows, chans), BF16),
            shape((rows, chans), F32),
            shape((stretches, modes, chans), F32),
            shape((length, modes, chans), F32),
        ),
        [pltpu.VMEM((streams, rows + RIM, chans), F32), pltpu.VMEM((rows, chans), F32)],
        8_000_000,
        2_000_000,
        [VMEM] * 6,
        "local",
    )(features, rim, short_weight, decay_rate, mode_gain, skip[None, :])
    everyone = lax.all_to_all(totals, CTX, split_axis=0, concat_axis=0, tiled=True)
    spread = call(
        join_kernel,
        shape((xs, ys, piece, rows), BF16),
        [pltpu.VMEM((stretches, modes, chans), F32), pltpu.VMEM((rows, chans), F32)],
        4_000_000,
        4_000_000,
        [SMEM] + [VMEM] * 6,
        "join",
    )(place.astype(jnp.int32).reshape(1), everyone, before, inner, query, table, decay_rate)
    gathered = lax.all_to_all(
        spread.reshape(xs * ys, piece, rows), CH, split_axis=0, concat_axis=0, tiled=True
    )
    partial = pl.pallas_call(
        project_kernel,
        out_shape=shape((xs, rows, wide), BF16),
        grid=(xs,),
        in_specs=[
            pl.BlockSpec((xs * ys, piece, rows), lambda i: (0, 0, 0)),
            pl.BlockSpec((length, 1, owned * piece, wide), lambda i: (0, i, 0, 0)),
        ],
        out_specs=pl.BlockSpec((1, rows, wide), lambda i: (i, 0, 0)),
        cost_estimate=pl.CostEstimate(
            flops=2 * rows * xs * ys * piece * wide * xs, bytes_accessed=6_000_000, transcendentals=0
        ),
        compiler_params=pltpu.CompilerParams(vmem_limit_bytes=32 << 20),
        name="project",
    )(gathered, weights)
    shares = lax.all_to_all(partial, "x", split_axis=0, concat_axis=0, tiled=True)
    total = shares[0].astype(F32)
    for i in range(1, xs):
        total = total + shares[i].astype(F32)
    return total.astype(BF16)


def solution(mesh):
    cores, xs = SHAPE["c"], SHAPE["x"]
    fine = Mesh(mesh.devices.reshape(-1, cores, xs, mesh.shape["ch"] // xs), ("z", "c", "x", "y"))
    return jax.shard_map(
        per_device,
        mesh=fine,
        in_specs=(
            P(None, CTX, CH),
            P(None, None, CH),
            P(CH, None),
            P(CH, None),
            P(CH),
            P(CTX, CH),
        ),
        out_specs=P(CTX, CH),
        check_vma=False,
    )
```

time: 196 us -> 120 us (0.61)
  the two profiles are of different devices: /device:TPU:4 before, /device:TPU:8 now
where the time goes in v1:
time: 120 us; the launch traced here: 119 us
  blocking collectives  61.3 us (51%)
  starting transfers between devices  14.9 us (12%)
  between operations  13.5 us (11%)
  waiting for transfers between devices  13 us (11%)
  local copies, waits for them, and re-layouts  8.43 us (7%)
  Pallas kernels  5.52 us (5%)
  other arithmetic  2.38 us (2%)
    all_to_all x1, blocking collectives, per_device(): lax.all_to_all(spread.reshape(xs * ys, piece, rows), CH, split_axis=0, co...  38 us
    all_to_all x1, starting transfers between devices, per_device(): lax.all_to_all(totals, CTX, split_axis=0, concat_axis=0, tiled=True)  13.6 us
    all_to_all x1, waiting for transfers between devices, per_device(): lax.all_to_all(totals, CTX, split_axis=0, concat_axis=0, tiled=True)  13 us
    all_to_all x1, blocking collectives, per_device(): lax.all_to_all(partial, 'x', split_axis=0, concat_axis=0, tiled=True)  12.4 us
    all_to_all x1, blocking collectives, per_device(): lax.all_to_all(sliced, 'x', split_axis=0, concat_axis=0, tiled=True)  10.9 us
    unnamed x14, local copies, waits for them, and re-layouts  6.75 us
    pallas_call x1, Pallas kernels, per_device(): call(local_kernel, (shape((rows, chans), BF16), shape((rows, chans), F32)...  2.6 us
  transfers between devices with their start and end apart: 3, of which 1 were waited for; matrix products, arithmetic and copies ran while one was open for 2% of the time, Pallas kernels for 3%

profile of v1, /device:TPU:8, one launch (start us, length us, event | category | flops | bytes accessed | tf_op | source)
XLA Modules:
  0.0 119.0 jit_solution(9308177297231935447)
XLA Ops:
  6.5 0.0 all-gather.3.cloned.1.call-start
  6.5 1.0 copy.8
  7.5 10.9 %all_to_all.20 = bf16[4,128,256]{2,1,0:T(8,128)(2,1)} all-to-all(bf16[4,128,256]{2,1,0:T(8,128)(2,1)S(1)} %bitcast.20), channel_id=1, replica_groups=mesh['z'=8,'c'=2,'x'=4,'y'=8] {'x'}, dimensions={0} | all-to-all | bytes 524288 | tf_op jit(solution)/shard_map/all_to_all | solution.py:142
  18.4 0.0 all-gather.3.cloned.1.call-update
  18.4 0.7 slice.15
  19.1 1.3 %collective-permute-start = (bf16[3,8,256]{2,1,0:T(8,128)(2,1)S(1)}, bf16[3,8,256]{2,1,0:T(8,128)(2,1)S(1)}, u32[]{:S(2)}, u32[]{:S(2)}) collective-permute-start(bf16[3,8,256]{2,1,0:T(8,128)(2,1)S(1)} %slice.15), channel_id=1, source_target_pairs={{0,32},{32,64},{64,96},{96,128},{128,160},{160,192},{192,224},{224... | collective-permute-start | bytes 36872 | tf_op jit(solution)/shard_map/ppermute | solution.py:136
  20.4 0.7 bitcast_negate_fusion
  21.1 0.9 exponential_multiply_fusion.table
  22.1 0.0 collective-permute-done.rim
  22.1 0.0 copy-start.1
  22.1 1.0 copy-done.1
  23.1 0.0 copy-start.2
  23.1 0.7 copy-done.2
  23.8 0.0 copy-start.4
  23.8 0.7 copy-done.4
  24.5 0.0 copy-start.5
  24.5 0.7 copy-done.5
  25.3 0.0 copy-start.6
  25.3 0.7 copy-done.6
  25.9 2.6 %local.1 = (bf16[256,256]{1,0:T(8,128)(2,1)S(1)}, f32[256,256]{1,0:T(8,128)S(1)}, f32[4,16,256]{2,1,0:T(8,128)S(1)}, f32[16,16,256]{2,1,0:T(8,128)}) custom-call(bf16[3,256,256]{2,1,0:T(8,128)(2,1)S(1)} %copy-done.1, bf16[3,8,256]{2,1,0:T(8,128)(2,1)S(1)} %collective-permute-done.rim, f32[3,7,256]{2,1,0:T(8,128)S(1)} %copy-done.5, f32[16,256]{1,0:T(8,128)S(1)} %bitcast.15, ...), custom_call_target="tpu_custom_call" | custom-call | flops 8000000 | bytes 2000000 | tf_op jit(solution)/shard_map/local/pallas_call | solution.py:150
  28.5 13.6 %all-to-all-start.1 = ((f32[16,16,256]{2,1,0:T(8,128)}), f32[16,16,256]{2,1,0:T(8,128)S(1)}, u32[]{:S(2)}, u32[]{:S(2)}) async-start(f32[16,16,256]{2,1,0:T(8,128)} %get-tuple-element.12), calls=%async_computation.1 | async-start | bytes 524288 | tf_op jit(solution)/shard_map/all_to_all | solution.py:164
  42.2 13.0 %all-to-all-done.1.everyone = f32[16,16,256]{2,1,0:T(8,128)S(1)} async-done(((f32[16,16,256]{2,1,0:T(8,128)}), f32[16,16,256]{2,1,0:T(8,128)S(1)}, u32[]{:S(2)}, u32[]{:S(2)}) %all-to-all-start.1) | async-done | bytes 262176 | tf_op jit(solution)/shard_map/all_to_all | solution.py:164
  55.2 0.0 copy-start.3
  55.2 0.7 copy-done.3
  55.9 0.7 join.1
  56.6 38.0 %all_to_all.21.gated = bf16[32,64,256]{2,1,0:T(8,128)(2,1)S(1)} all-to-all(bf16[32,64,256]{2,1,0:T(8,128)(2,1)S(1)} %bitcast.13), channel_id=1, replica_groups=mesh['z'=8,'c'=2,'x'=4,'y'=8] {'x','y'}, dimensions={0} | all-to-all | bytes 2097152 | tf_op jit(solution)/shard_map/all_to_all | solution.py:174
  94.6 0.0 all-gather.3.cloned.1.call-done
  94.6 0.0 copy-start
  94.6 2.2 %copy-done = bf16[64,128,256]{2,1,0:T(8,128)(2,1)S(1)} copy-done((bf16[64,128,256]{2,1,0:T(8,128)(2,1)S(1)}, bf16[64,128,256]{2,1,0:T(8,128)(2,1)}, u32[]{:S(2)}) %copy-start) | copy-done | bytes 4194328
  96.8 2.3 %project.1 = bf16[4,256,256]{2,1,0:T(8,128)(2,1)S(1)} custom-call(bf16[32,64,256]{2,1,0:T(8,128)(2,1)S(1)} %all_to_all.21.gated, bf16[16,4,128,256]{3,2,1,0:T(8,128)(2,1)S(1)} %bitcast.14), custom_call_target="tpu_custom_call" | custom-call | flops 1073741824 | bytes 6000000 | tf_op jit(solution)/shard_map/project/pallas_call | solution.py:177
  99.0 12.4 %all_to_all.22 = bf16[4,256,256]{2,1,0:T(8,128)(2,1)S(1)} all-to-all(bf16[4,256,256]{2,1,0:T(8,128)(2,1)S(1)} %project.1), channel_id=1, replica_groups=mesh['z'=8,'c'=2,'x'=4,'y'=8] {'x'}, dimensions={0} | all-to-all | bytes 1048576 | tf_op jit(solution)/shard_map/all_to_all | solution.py:192
  111.5 0.7 fusion
  (1 shorter events, 0.0 us)
Async XLA Ops:
  6.5 88.0 %all-gather.3.cloned.1.call-start = ((), (), s32[]{:S(2)}) async-start(), calls=%async_computation.4 | async-start | bytes 4456448 | tf_op jit(solution)/shard_map/all_gather | solution.py:143
  19.1 3.0 %collective-permute-start = (bf16[3,8,256]{2,1,0:T(8,128)(2,1)S(1)}, bf16[3,8,256]{2,1,0:T(8,128)(2,1)S(1)}, u32[]{:S(2)}, u32[]{:S(2)}) collective-permute-start(bf16[3,8,256]{2,1,0:T(8,128)(2,1)S(1)} %slice.15), channel_id=1, source_target_pairs={{0,32},{32,64},{64,96},{96,128},{128,160},{160,192},{192,224},{224... | collective-permute-start | bytes 36872 | tf_op jit(solution)/shard_map/ppermute | solution.py:136
  22.1 1.0 copy-start.1
  23.1 0.7 copy-start.2
  23.8 0.7 copy-start.4
  24.5 0.7 copy-start.5
  25.3 0.7 copy-start.6
  28.5 26.6 %all-to-all-start.1 = ((f32[16,16,256]{2,1,0:T(8,128)}), f32[16,16,256]{2,1,0:T(8,128)S(1)}, u32[]{:S(2)}, u32[]{:S(2)}) async-start(f32[16,16,256]{2,1,0:T(8,128)} %get-tuple-element.12), calls=%async_computation.1 | async-start | bytes 524288 | tf_op jit(solution)/shard_map/all_to_all | solution.py:164
  55.2 0.7 copy-start.3
  94.6 2.2 %copy-start = (bf16[64,128,256]{2,1,0:T(8,128)(2,1)S(1)}, bf16[64,128,256]{2,1,0:T(8,128)(2,1)}, u32[]{:S(2)}) copy-start(bf16[64,128,256]{2,1,0:T(8,128)(2,1)} %all-gather.3.cloned.1.call-done) | copy-start | bytes 12582916
Sparse Core Ops, SparseCore 0:
  18.5 52.4 all-gather.2

commit v2 on v1

v2 whole, which is shorter than its diff:
```python
import jax
import jax.numpy as jnp
from jax import lax
from jax.experimental import pallas as pl
from jax.experimental.pallas import tpu as pltpu
from jax.sharding import Mesh
from jax.sharding import PartitionSpec as P


STRETCH = 64
RIM = 8
SHAPE = {"c": 2, "x": 4}
F32 = jnp.float32
BF16 = jnp.bfloat16
CTX = ("z", "c")
CH = ("x", "y")
VMEM = pl.BlockSpec(memory_space=pltpu.VMEM)
SMEM = pl.BlockSpec(memory_space=pltpu.SMEM)


def local_kernel(
    features_at, taps_at, rates_at, gains_at, skip_at, rim, query, inner, before, decays, totals,
    features, taps, rates, gains, skip, sems, extended, product,
):
    pairs = ((features_at, features), (taps_at, taps), (rates_at, rates), (gains_at, gains), (skip_at, skip))
    copies = [pltpu.make_async_copy(src, dst, sems.at[i]) for i, (src, dst) in enumerate(pairs)]
    for copy in copies:
        copy.start()
    for copy in copies:
        copy.wait()
    streams, rows, chans = features.shape
    width = taps.shape[1]
    modes = rates.shape[0]
    stretches = rows // STRETCH
    piece = 32
    for f in range(streams):
        extended[f, 0:RIM, :] = rim[f].astype(F32)
        extended[f, RIM : RIM + rows, :] = features[f].astype(F32)
    for start in range(0, rows, piece):
        parts = []
        for f in range(streams):
            total = jnp.zeros((piece, chans), F32)
            for offset in range(width):
                at = RIM + start - offset
                total = total + taps[f, offset : offset + 1, :] * extended[f, at : at + piece, :]
            parts.append(total.astype(BF16))
        query[start : start + piece, :] = parts[0]
        product[start : start + piece, :] = (
            (parts[1].astype(F32) * parts[2].astype(F32)).astype(BF16).astype(F32)
        )
    decay = jnp.exp(-rates[...])
    gain = gains[...]
    through = skip[...]

    def eight(i, states):
        states = list(states)
        base = pl.multiple_of(i * 8, 8)
        for k in range(stretches):
            at = pl.multiple_of(k * STRETCH + base, 8)
            tile = product[pl.ds(at, 8), :]
            outs = []
            state = states[k]
            for r in range(8):
                state = decay * state + jnp.broadcast_to(tile[r : r + 1, :], (modes, chans))
                outs.append(jnp.sum(gain * state, axis=0, keepdims=True))
            states[k] = state
            inner[pl.ds(at, 8), :] = jnp.concatenate(outs, axis=0) + through * tile
        return tuple(states)

    zero = jnp.zeros((modes, chans), F32)
    states = lax.fori_loop(0, STRETCH // 8, eight, (zero,) * stretches)
    for k in range(stretches + 1):
        decays[k] = jnp.exp(-rates[...] * (k * STRETCH))
    across = decays[1]
    running = zero
    for k in range(stretches):
        before[k] = running
        running = across * running + states[k]
    totals[...] = running


def join_kernel(place, everyone, pair, before, decays, inner, query, table, out, starts, gated):
    chips, modes, chans = everyone.shape
    stretches = before.shape[0]
    span = decays[stretches]
    chip_span = span * span
    incoming = jnp.zeros((modes, chans), F32)
    for i in range(chips):
        incoming = jnp.where(i < place[0], chip_span * incoming + everyone[i], incoming)
    incoming = jnp.where(place[1] > 0, span * incoming + pair[0], incoming)
    for k in range(stretches):
        starts[k] = decays[k] * incoming + before[k]

    def eight(i, carry):
        base = pl.multiple_of(i * 8, 8)
        totals = [inner[pl.ds(pl.multiple_of(k * STRETCH + base, 8), 8), :] for k in range(stretches)]
        for n in range(modes):
            weight = table[n, pl.ds(base, 8), :]
            for k in range(stretches):
                totals[k] = totals[k] + weight * starts[k, n : n + 1, :]
        for k in range(stretches):
            at = pl.multiple_of(k * STRETCH + base, 8)
            gated[pl.ds(at, 8), :] = query[pl.ds(at, 8), :].astype(F32) * totals[k]
        return carry

    lax.fori_loop(0, STRETCH // 8, eight, 0)
    turned = gated[...].T.astype(BF16)
    blocks = out.shape[0]
    height = out.shape[2]
    for b in range(blocks):
        for copy in range(out.shape[1]):
            out[b, copy] = turned[b * height : (b + 1) * height, :]


def project_kernel(gated, weight, out):
    depth = gated.shape[0] * gated.shape[1]
    left = gated[...].reshape(depth, gated.shape[2])
    right = weight[...].reshape(depth, weight.shape[3])
    out[0] = lax.dot_general(left, right, (((0,), (0,)), ((), ())), preferred_element_type=F32).astype(BF16)


def whole(value):
    return pl.BlockSpec(value.shape, lambda i: (0,) * value.ndim)


def mixed_of(features, short_weight, rates, residues, skip, out_weight):
    streams, rows, chans = features.shape
    modes = rates.shape[1]
    length = lax.axis_size(CTX)
    zs, xs, ys = lax.axis_size("z"), lax.axis_size("x"), lax.axis_size("y")
    place = jnp.stack([lax.axis_index("z"), lax.axis_index("c")]).astype(jnp.int32)
    decay_rate = rates.T
    mode_gain = residues.T
    shape = jax.ShapeDtypeStruct

    deep, wide = out_weight.shape
    owned = deep // chans
    piece = chans // xs
    height = owned * piece
    sliced = out_weight.reshape(owned, xs, piece, wide).transpose(1, 0, 2, 3).reshape(xs, height, wide)
    sliced = lax.all_to_all(sliced, "x", split_axis=0, concat_axis=0, tiled=True)
    weights = lax.all_gather(sliced, CTX, axis=0, tiled=False)

    rim = lax.ppermute(features[:, rows - RIM :, :], CTX, [(i, i + 1) for i in range(length - 1)])
    lag = jnp.arange(STRETCH, dtype=F32) + 1.0
    table = mode_gain[:, None, :] * jnp.exp(-decay_rate[:, None, :] * lag[None, :, None])
    rim, table, place = lax.optimization_barrier((rim, table, place))

    stretches = rows // STRETCH
    shapes = (
        shape((rows, chans), BF16),
        shape((rows, chans), F32),
        shape((stretches, modes, chans), F32),
        shape((stretches + 1, modes, chans), F32),
        shape((modes, chans), F32),
    )
    operands = (features, short_weight, decay_rate, mode_gain, skip[None, :])
    query, inner, before, decays, totals = pl.pallas_call(
        local_kernel,
        out_shape=shapes,
        in_specs=[pl.BlockSpec(memory_space=pltpu.HBM)] * len(operands) + [VMEM],
        out_specs=(VMEM,) * len(shapes),
        scratch_shapes=[pltpu.VMEM(v.shape, v.dtype) for v in operands]
        + [
            pltpu.SemaphoreType.DMA((len(operands),)),
            pltpu.VMEM((streams, rows + RIM, chans), F32),
            pltpu.VMEM((rows, chans), F32),
        ],
        cost_estimate=pl.CostEstimate(flops=8_000_000, bytes_accessed=2_000_000, transcendentals=0),
        compiler_params=pltpu.CompilerParams(vmem_limit_bytes=32 << 20),
        name="local",
    )(*operands, rim)
    pair = lax.all_gather(totals, "c", axis=0, tiled=False)
    chip = decays[stretches] * pair[0] + pair[1]
    everyone = lax.all_to_all(
        jnp.broadcast_to(chip[None], (zs, modes, chans)), "z", split_axis=0, concat_axis=0, tiled=True
    )
    spread = pl.pallas_call(
        join_kernel,
        out_shape=shape((xs, ys, piece, rows), BF16),
        in_specs=[SMEM] + [VMEM] * 7,
        out_specs=VMEM,
        scratch_shapes=[pltpu.VMEM((stretches, modes, chans), F32), pltpu.VMEM((rows, chans), F32)],
        cost_estimate=pl.CostEstimate(flops=4_000_000, bytes_accessed=4_000_000, transcendentals=0),
        compiler_params=pltpu.CompilerParams(vmem_limit_bytes=32 << 20),
        name="join",
    )(place, everyone, pair, before, decays, inner, query, table)
    gathered = lax.all_to_all(
        spread.reshape(xs * ys, piece, rows), CH, split_axis=0, concat_axis=0, tiled=True
    )
    partial = pl.pallas_call(
        project_kernel,
        out_shape=shape((xs, rows, wide), BF16),
        grid=(xs,),
        in_specs=[
            whole(gathered),
            pl.BlockSpec((length, 1, height, wide), lambda i: (0, i, 0, 0)),
        ],
        out_specs=pl.BlockSpec((1, rows, wide), lambda i: (i, 0, 0)),
        cost_estimate=pl.CostEstimate(
            flops=2 * rows * length * height * wide * xs, bytes_accessed=6_000_000, transcendentals=0
        ),
        compiler_params=pltpu.CompilerParams(vmem_limit_bytes=60 << 20),
        name="project",
    )(gathered, weights)
    shares = lax.all_to_all(partial, "x", split_axis=0, concat_axis=0, tiled=True)
    total = shares[0].astype(F32)
    for i in range(1, xs):
        total = total + shares[i].astype(F32)
    return total.astype(BF16)


def solution(mesh):
    cores, xs = SHAPE["c"], SHAPE["x"]
    fine = Mesh(mesh.devices.reshape(-1, cores, xs, mesh.shape["ch"] // xs), ("z", "c", "x", "y"))
    return jax.shard_map(
        mixed_of,
        mesh=fine,
        in_specs=(
            P(None, CTX, CH),
            P(None, None, CH),
            P(CH, None),
            P(CH, None),
            P(CH),
            P(CTX, CH),
        ),
        out_specs=P(CTX, CH),
        check_vma=False,
    )
```

time: 120 us -> 116 us (0.967)
  blocking collectives: 61.3 us -> 84 us
  starting transfers between devices: 14.9 us -> 1.28 us
  waiting for transfers between devices: 13 us -> 0.02 us
  Pallas kernels: 5.52 us -> 8.49 us
  local copies, waits for them, and re-layouts: 8.43 us -> 5.54 us
    all_to_all x3 -> x4, blocking collectives: 61.3 us -> 79.4 us  [the longest x1 35.5 us: mixed_of(): lax.all_to_all(spread.reshape(xs * ys, piece, rows), CH, split_axis=0, co...]
    all_to_all x1 -> x0, starting transfers between devices: 13.6 us -> none  [per_device(): lax.all_to_all(totals, CTX, split_axis=0, concat_axis=0, tiled=True)]
    all_to_all x1 -> x0, waiting for transfers between devices: 13 us -> none  [per_device(): lax.all_to_all(totals, CTX, split_axis=0, concat_axis=0, tiled=True)]
    all_gather x0 -> x1, blocking collectives: none -> 4.59 us  [mixed_of(): pair = lax.all_gather(totals, 'c', axis=0, tiled=False)]
    pallas_call x3, Pallas kernels: 5.52 us -> 8.49 us  [the longest x1 5.12 us: mixed_of(): pl.pallas_call(project_kernel, out_shape=shape((xs, rows, wide), BF16), g...]
    unnamed x14 -> x10, local copies, waits for them, and re-layouts: 6.75 us -> 3.85 us
  transfers between devices with their start and end apart: 3 -> 2, of which waited for: 1 -> 0; matrix products, arithmetic and copies ran while one was open for 2% -> 2% of each run, Pallas kernels for 3% -> 3%
where the time goes in v2:
time: 116 us; the launch traced here: 115 us
  blocking collectives  84 us (72%)
  between operations  13.4 us (12%)
  Pallas kernels  8.49 us (7%)
  local copies, waits for them, and re-layouts  5.54 us (5%)
  other arithmetic  2.46 us (2%)
  starting transfers between devices  1.28 us (1%)
    all_to_all x1, blocking collectives, mixed_of(): lax.all_to_all(spread.reshape(xs * ys, piece, rows), CH, split_axis=0, co...  35.5 us
    all_to_all x1, blocking collectives, mixed_of(): lax.all_to_all(jnp.broadcast_to(chip[None], (zs, modes, chans)), 'z', spl...  21.6 us
    all_to_all x1, blocking collectives, mixed_of(): lax.all_to_all(partial, 'x', split_axis=0, concat_axis=0, tiled=True)  11.5 us
    all_to_all x1, blocking collectives, mixed_of(): lax.all_to_all(sliced, 'x', split_axis=0, concat_axis=0, tiled=True)  10.9 us
    pallas_call x1, Pallas kernels, mixed_of(): pl.pallas_call(project_kernel, out_shape=shape((xs, rows, wide), BF16), g...  5.12 us
    all_gather x1, blocking collectives, mixed_of(): pair = lax.all_gather(totals, 'c', axis=0, tiled=False)  4.59 us
    unnamed x10, local copies, waits for them, and re-layouts  3.85 us
  transfers between devices with their start and end apart: 2, of which 0 were waited for; matrix products, arithmetic and copies ran while one was open for 2% of the time, Pallas kernels for 3%

profile of v2, /device:TPU:8, one launch (start us, length us, event | category | flops | bytes accessed | tf_op | source)
XLA Modules:
  0.0 115.3 jit_solution(10949946699588904037)
XLA Ops:
  6.5 0.0 all-gather.4.cloned.1.call-start
  6.5 1.0 copy.8
  7.5 10.9 %all_to_all.20 = bf16[4,128,256]{2,1,0:T(8,128)(2,1)} all-to-all(bf16[4,128,256]{2,1,0:T(8,128)(2,1)S(1)} %bitcast.36), channel_id=1, replica_groups=mesh['z'=8,'c'=2,'x'=4,'y'=8] {'x'}, dimensions={0} | all-to-all | bytes 524288 | tf_op jit(solution)/shard_map/all_to_all | solution.py:141
  18.4 0.0 all-gather.4.cloned.1.call-update
  18.4 0.7 slice.24
  19.1 1.3 %collective-permute-start = (bf16[3,8,256]{2,1,0:T(8,128)(2,1)S(1)}, bf16[3,8,256]{2,1,0:T(8,128)(2,1)S(1)}, u32[]{:S(2)}, u32[]{:S(2)}) collective-permute-start(bf16[3,8,256]{2,1,0:T(8,128)(2,1)S(1)} %slice.24), channel_id=1, source_target_pairs={{0,32},{32,64},{64,96},{96,128},{128,160},{160,192},{192,224},{224... | collective-permute-start | bytes 36872 | tf_op jit(solution)/shard_map/ppermute | solution.py:144
  20.4 0.7 bitcast_negate_fusion
  21.2 0.9 exponential_multiply_fusion.table
  22.1 0.1 pad_add_fusion.place
  22.2 0.0 collective-permute-done.rim
  22.2 0.0 copy-start
  22.2 1.0 copy-done
  23.2 0.0 copy-start.1
  23.2 0.7 copy-done.1
  23.9 0.0 copy-start.2
  23.9 0.7 copy-done.2
  24.6 0.0 copy-start.3
  24.6 0.7 copy-done.3
  25.3 0.0 copy-start.4
  25.3 0.7 copy-done.4
  26.0 2.2 %local.1 = (bf16[256,256]{1,0:T(8,128)(2,1)S(1)}, f32[256,256]{1,0:T(8,128)S(1)}, f32[4,16,256]{2,1,0:T(8,128)S(1)}, f32[5,16,256]{2,1,0:T(8,128)S(1)}, f32[16,256]{1,0:T(8,128)S(1)}) custom-call(bf16[3,256,256]{2,1,0:T(8,128)(2,1)S(1)} %copy-done, f32[3,7,256]{2,1,0:T(8,128)S(1)} %copy-done.3, f32[16,256]{1,0:T(8,128)S(1)} %bitcast.33, ...), custom_call_target="tpu_custom_call" | custom-call | flops 8000000 | bytes 2000000 | tf_op jit(solution)/shard_map/local/pallas_call | solution.py:158
  28.2 4.6 %all-gather = f32[32,256]{1,0:T(8,128)S(1)} all-gather(f32[16,256]{1,0:T(8,128)S(1)} %get-tuple-element.16), channel_id=2, replica_groups=mesh['z'=8,'c'=2,'x'=4,'y'=8] {'c'}, dimensions={0}, use_global_device_ids=true | all-gather | bytes 49152 | tf_op jit(solution)/shard_map/all_gather | solution.py:173
  32.8 21.6 %all_to_all.21.everyone = f32[8,16,256]{2,1,0:T(8,128)S(1)} all-to-all(f32[8,16,256]{2,1,0:T(8,128)S(1)} %broadcast_in_dim.16), channel_id=1, replica_groups=mesh['z'=8,'c'=2,'x'=4,'y'=8] {'z'}, dimensions={0} | all-to-all | bytes 262144 | tf_op jit(solution)/shard_map/all_to_all | solution.py:175
  54.4 1.2 %join.1 = bf16[4,8,64,256]{3,2,1,0:T(8,128)(2,1)S(1)} custom-call(s32[2]{0:T(128)S(1)} %pad_add_fusion.place, f32[8,16,256]{2,1,0:T(8,128)S(1)} %all_to_all.21.everyone, f32[2,16,256]{2,1,0:T(8,128)S(1)} %bitcast.30, f32[4,16,256]{2,1,0:T(8,128)S(1)} %get-tuple-element.17.before, f32[5,16,256]{2,1,0:T(8,128)S(1)} %get-tuple-element.15.decays, ...), custom_call_target="tpu_custom_call" | custom-call | flops 4000000 | bytes 4000000 | tf_op jit(solution)/shard_map/join/pallas_call | solution.py:178
  55.6 35.5 %all_to_all.22.gated = bf16[32,64,256]{2,1,0:T(8,128)(2,1)} all-to-all(bf16[32,64,256]{2,1,0:T(8,128)(2,1)S(1)} %bitcast.29), channel_id=1, replica_groups=mesh['z'=8,'c'=2,'x'=4,'y'=8] {'x','y'}, dimensions={0} | all-to-all | bytes 2097152 | tf_op jit(solution)/shard_map/all_to_all | solution.py:188
  91.0 0.0 all-gather.4.cloned.1.call-done
  91.1 5.1 %project.1 = bf16[4,256,256]{2,1,0:T(8,128)(2,1)} custom-call(bf16[32,64,256]{2,1,0:T(8,128)(2,1)} %all_to_all.22.gated, bf16[16,4,128,256]{3,2,1,0:T(8,128)(2,1)} %bitcast.35), custom_call_target="tpu_custom_call" | custom-call | flops 1073741824 | bytes 6000000 | tf_op jit(solution)/shard_map/project/pallas_call | solution.py:191
  96.2 11.5 %all_to_all.23 = bf16[4,256,256]{2,1,0:T(8,128)(2,1)S(1)} all-to-all(bf16[4,256,256]{2,1,0:T(8,128)(2,1)} %project.1), channel_id=1, replica_groups=mesh['z'=8,'c'=2,'x'=4,'y'=8] {'x'}, dimensions={0} | all-to-all | bytes 1048576 | tf_op jit(solution)/shard_map/all_to_all | solution.py:206
  107.7 0.7 fusion
  (3 shorter events, 0.0 us)
Async XLA Ops:
  6.5 84.5 %all-gather.4.cloned.1.call-start = ((), (), s32[]{:S(2)}) async-start(), calls=%async_computation.4 | async-start | bytes 4456448 | tf_op jit(solution)/shard_map/all_gather | solution.py:142
  19.1 3.0 %collective-permute-start = (bf16[3,8,256]{2,1,0:T(8,128)(2,1)S(1)}, bf16[3,8,256]{2,1,0:T(8,128)(2,1)S(1)}, u32[]{:S(2)}, u32[]{:S(2)}) collective-permute-start(bf16[3,8,256]{2,1,0:T(8,128)(2,1)S(1)} %slice.24), channel_id=1, source_target_pairs={{0,32},{32,64},{64,96},{96,128},{128,160},{160,192},{192,224},{224... | collective-permute-start | bytes 36872 | tf_op jit(solution)/shard_map/ppermute | solution.py:144
  22.2 1.0 copy-start
  23.2 0.7 copy-start.1
  23.9 0.7 copy-start.2
  24.6 0.7 copy-start.3
  25.3 0.7 copy-start.4
Sparse Core Ops, SparseCore 0:
  18.5 49.9 all-gather.3

commit v3 on v2

--- a/solution.py
+++ b/solution.py
@@ -8,6 +8,7 @@
 
 
 STRETCH = 64
+TILE = 8
 RIM = 8
 SHAPE = {"c": 2, "x": 4}
 F32 = jnp.float32
@@ -19,19 +20,27 @@
 
 
 def local_kernel(
-    features_at, taps_at, rates_at, gains_at, skip_at, rim, query, inner, before, decays, totals,
+    features_at, taps_at, rates_at, gains_at, skip_at, rim, query, inner, before, decays, slope, totals,
     features, taps, rates, gains, skip, sems, extended, product,
 ):
-    pairs = ((features_at, features), (taps_at, taps), (rates_at, rates), (gains_at, gains), (skip_at, skip))
+    pairs = ((rates_at, rates), (gains_at, gains), (features_at, features), (taps_at, taps), (skip_at, skip))
     copies = [pltpu.make_async_copy(src, dst, sems.at[i]) for i, (src, dst) in enumerate(pairs)]
     for copy in copies:
         copy.start()
-    for copy in copies:
-        copy.wait()
     streams, rows, chans = features.shape
     width = taps.shape[1]
     modes = rates.shape[0]
     stretches = rows // STRETCH
+    for copy in copies[:2]:
+        copy.wait()
+    for k in range(stretches + 1):
+        decays[k] = jnp.exp(-rates[...] * (k * STRETCH))
+    decays[stretches + 1] = jnp.exp(-rates[...] * TILE)
+    lags = lax.broadcasted_iota(jnp.int32, (TILE, chans), 0).astype(F32) + 1.0
+    for n in range(modes):
+        slope[n] = gains[n : n + 1, :] * jnp.exp(-rates[n : n + 1, :] * lags)
+    for copy in copies[2:]:
+        copy.wait()
     piece = 32
     for f in range(streams):
         extended[f, 0:RIM, :] = rim[f].astype(F32)
@@ -69,8 +78,6 @@
 
     zero = jnp.zeros((modes, chans), F32)
     states = lax.fori_loop(0, STRETCH // 8, eight, (zero,) * stretches)
-    for k in range(stretches + 1):
-        decays[k] = jnp.exp(-rates[...] * (k * STRETCH))
     across = decays[1]
     running = zero
     for k in range(stretches):
@@ -79,7 +86,7 @@
     totals[...] = running
 
 
-def join_kernel(place, everyone, pair, before, decays, inner, query, table, out, starts, gated):
+def join_kernel(place, everyone, pair, before, decays, slope, inner, query, out, starts, gated, table):
     chips, modes, chans = everyone.shape
     stretches = before.shape[0]
     span = decays[stretches]
@@ -91,11 +98,14 @@
     for k in range(stretches):
         starts[k] = decays[k] * incoming + before[k]
 
+    table[...] = slope[...]
+
     def eight(i, carry):
         base = pl.multiple_of(i * 8, 8)
         totals = [inner[pl.ds(pl.multiple_of(k * STRETCH + base, 8), 8), :] for k in range(stretches)]
         for n in range(modes):
-            weight = table[n, pl.ds(base, 8), :]
+            weight = table[n]
+            table[n] = weight * decays[stretches + 1, n : n + 1, :]
             for k in range(stretches):
                 totals[k] = totals[k] + weight * starts[k, n : n + 1, :]
         for k in range(stretches):
@@ -112,15 +122,17 @@
             out[b, copy] = turned[b * height : (b + 1) * height, :]
 
 
-def project_kernel(gated, weight, out):
+def project_kernel(gated, weight_at, out, weight, sems):
+    parts = out.shape[0]
+    copies = [pltpu.make_async_copy(weight_at.at[:, i], weight.at[i], sems.at[i]) for i in range(parts)]
+    for copy in copies:
+        copy.start()
     depth = gated.shape[0] * gated.shape[1]
-    left = gated[...].reshape(depth, gated.shape[2])
-    right = weight[...].reshape(depth, weight.shape[3])
-    out[0] = lax.dot_general(left, right, (((0,), (0,)), ((), ())), preferred_element_type=F32).astype(BF16)
-
-
-def whole(value):
-    return pl.BlockSpec(value.shape, lambda i: (0,) * value.ndim)
+    left = gated[...].reshape(depth, gated.shape[2]).T
+    for i in range(parts):
+        copies[i].wait()
+        right = weight[i].reshape(depth, weight.shape[3])
+        out[i] = jnp.dot(left, right, preferred_element_type=F32).astype(BF16)
 
 
 def mixed_of(features, short_weight, rates, residues, skip, out_weight):
@@ -142,23 +154,22 @@
     weights = lax.all_gather(sliced, CTX, axis=0, tiled=False)
 
     rim = lax.ppermute(features[:, rows - RIM :, :], CTX, [(i, i + 1) for i in range(length - 1)])
-    lag = jnp.arange(STRETCH, dtype=F32) + 1.0
-    table = mode_gain[:, None, :] * jnp.exp(-decay_rate[:, None, :] * lag[None, :, None])
-    rim, table, place = lax.optimization_barrier((rim, table, place))
+    rim, place = lax.optimization_barrier((rim, place))
 
     stretches = rows // STRETCH
     shapes = (
         shape((rows, chans), BF16),
         shape((rows, chans), F32),
         shape((stretches, modes, chans), F32),
-        shape((stretches + 1, modes, chans), F32),
+        shape((stretches + 2, modes, chans), F32),
+        shape((modes, TILE, chans), F32),
         shape((modes, chans), F32),
     )
     operands = (features, short_weight, decay_rate, mode_gain, skip[None, :])
-    query, inner, before, decays, totals = pl.pallas_call(
+    query, inner, before, decays, slope, totals = pl.pallas_call(
         local_kernel,
         out_shape=shapes,
-        in_specs=[pl.BlockSpec(memory_space=pltpu.HBM)] * len(operands) + [VMEM],
+        in_specs=[pl.BlockSpec(memory_space=pl.ANY)] * len(operands) + [VMEM],
         out_specs=(VMEM,) * len(shapes),
         scratch_shapes=[pltpu.VMEM(v.shape, v.dtype) for v in operands]
         + [
@@ -167,7 +178,7 @@
             pltpu.VMEM((rows, chans), F32),
         ],
         cost_estimate=pl.CostEstimate(flops=8_000_000, bytes_accessed=2_000_000, transcendentals=0),
-        compiler_params=pltpu.CompilerParams(vmem_limit_bytes=32 << 20),
+        compiler_params=pltpu.CompilerParams(vmem_limit_bytes=60 << 20),
         name="local",
     )(*operands, rim)
     pair = lax.all_gather(totals, "c", axis=0, tiled=False)
@@ -180,27 +191,31 @@
         out_shape=shape((xs, ys, piece, rows), BF16),
         in_specs=[SMEM] + [VMEM] * 7,
         out_specs=VMEM,
-        scratch_shapes=[pltpu.VMEM((stretches, modes, chans), F32), pltpu.VMEM((rows, chans), F32)],
+        scratch_shapes=[
+            pltpu.VMEM((stretches, modes, chans), F32),
+            pltpu.VMEM((rows, chans), F32),
+            pltpu.VMEM((modes, TILE, chans), F32),
+        ],
         cost_estimate=pl.CostEstimate(flops=4_000_000, bytes_accessed=4_000_000, transcendentals=0),
         compiler_params=pltpu.CompilerParams(vmem_limit_bytes=32 << 20),
         name="join",
-    )(place, everyone, pair, before, decays, inner, query, table)
+    )(place, everyone, pair, before, decays, slope, inner, query)
     gathered = lax.all_to_all(
         spread.reshape(xs * ys, piece, rows), CH, split_axis=0, concat_axis=0, tiled=True
     )
     partial = pl.pallas_call(
         project_kernel,
         out_shape=shape((xs, rows, wide), BF16),
-        grid=(xs,),
-        in_specs=[
-            whole(gathered),
-            pl.BlockSpec((length, 1, height, wide), lambda i: (0, i, 0, 0)),
+        in_specs=[VMEM, pl.BlockSpec(memory_space=pl.ANY)],
+        out_specs=VMEM,
+        scratch_shapes=[
+            pltpu.VMEM((xs, length, height, wide), BF16),
+            pltpu.SemaphoreType.DMA((xs,)),
         ],
-        out_specs=pl.BlockSpec((1, rows, wide), lambda i: (i, 0, 0)),
         cost_estimate=pl.CostEstimate(
             flops=2 * rows * length * height * wide * xs, bytes_accessed=6_000_000, transcendentals=0
         ),
-        compiler_params=pltpu.CompilerParams(vmem_limit_bytes=60 << 20),
+        compiler_params=pltpu.CompilerParams(vmem_limit_bytes=58 << 20),
         name="project",
     )(gathered, weights)
     shares = lax.all_to_all(partial, "x", split_axis=0, concat_axis=0, tiled=True)

time: 116 us -> 121 us (1.043)
  Pallas kernels: 8.49 us -> 11.7 us
  local copies, waits for them, and re-layouts: 5.54 us -> 6.78 us
    pallas_call x1, Pallas kernels: 2.18 us -> 4.43 us  [mixed_of(): pl.pallas_call(local_kernel, out_shape=shapes, in_specs=[pl.BlockSpec(mem...]
    unnamed x10 -> x12, local copies, waits for them, and re-layouts: 3.85 us -> 5.09 us
  transfers between devices with their start and end apart: 2 -> 2, of which waited for: 0 -> 1; matrix products, arithmetic and copies ran while one was open for 2% -> 1% of each run, Pallas kernels for 3% -> 5%
where the time goes in v3:
time: 121 us
  blocking collectives  85.1 us (70%)
  between operations  13.4 us (11%)
  Pallas kernels  11.7 us (10%)
  local copies, waits for them, and re-layouts  6.78 us (6%)
  other arithmetic  1.52 us (1%)
  starting transfers between devices  1.28 us (1%)
    all_to_all x1, blocking collectives, mixed_of(): lax.all_to_all(spread.reshape(xs * ys, piece, rows), CH, split_axis=0, co...  35.4 us
    all_to_all x1, blocking collectives, mixed_of(): lax.all_to_all(jnp.broadcast_to(chip[None], (zs, modes, chans)), 'z', spl...  22.5 us
    all_to_all x1, blocking collectives, mixed_of(): lax.all_to_all(partial, 'x', split_axis=0, concat_axis=0, tiled=True)  11.5 us
    all_to_all x1, blocking collectives, mixed_of(): lax.all_to_all(sliced, 'x', split_axis=0, concat_axis=0, tiled=True)  10.9 us
    pallas_call x1, Pallas kernels, mixed_of(): pl.pallas_call(project_kernel, out_shape=shape((xs, rows, wide), BF16), i...  6.09 us
    unnamed x12, local copies, waits for them, and re-layouts  5.09 us
    all_gather x1, blocking collectives, mixed_of(): pair = lax.all_gather(totals, 'c', axis=0, tiled=False)  4.79 us
    pallas_call x1, Pallas kernels, mixed_of(): pl.pallas_call(local_kernel, out_shape=shapes, in_specs=[pl.BlockSpec(mem...  4.43 us
  transfers between devices with their start and end apart: 2, of which 1 were waited for; matrix products, arithmetic and copies ran while one was open for 1% of the time, Pallas kernels for 5%

profile of v3, /device:TPU:8, one launch (start us, length us, event | category | flops | bytes accessed | tf_op | source)
XLA Modules:
  0.0 120.6 jit_solution(14855873014375170791)
XLA Ops:
  6.5 0.0 all-gather.4.cloned.1.call-start
  6.5 1.0 copy.8
  7.5 10.9 %all_to_all.20 = bf16[4,128,256]{2,1,0:T(8,128)(2,1)} all-to-all(bf16[4,128,256]{2,1,0:T(8,128)(2,1)S(1)} %bitcast.31), channel_id=1, replica_groups=mesh['z'=8,'c'=2,'x'=4,'y'=8] {'x'}, dimensions={0} | all-to-all | bytes 524288 | tf_op jit(solution)/shard_map/all_to_all | solution.py:153
  18.4 0.0 all-gather.4.cloned.1.call-update
  18.4 0.7 slice.24
  19.1 1.3 %collective-permute-start = (bf16[3,8,256]{2,1,0:T(8,128)(2,1)S(1)}, bf16[3,8,256]{2,1,0:T(8,128)(2,1)S(1)}, u32[]{:S(2)}, u32[]{:S(2)}) collective-permute-start(bf16[3,8,256]{2,1,0:T(8,128)(2,1)S(1)} %slice.24), channel_id=1, source_target_pairs={{0,32},{32,64},{64,96},{96,128},{128,160},{160,192},{192,224},{224... | collective-permute-start | bytes 36872 | tf_op jit(solution)/shard_map/ppermute | solution.py:156
  20.4 0.1 pad_add_fusion.place
  20.5 0.7 collective-permute-done.rim
  21.2 0.0 copy-start.5
  21.2 0.6 copy-done.5
  21.8 4.4 %local.1 = (bf16[256,256]{1,0:T(8,128)(2,1)}, f32[256,256]{1,0:T(8,128)}, f32[4,16,256]{2,1,0:T(8,128)}, f32[6,16,256]{2,1,0:T(8,128)}, f32[16,8,256]{2,1,0:T(8,128)}, /*index=5*/f32[16,256]{1,0:T(8,128)}) custom-call(bf16[3,256,256]{2,1,0:T(8,128)(2,1)} %features_at.1, f32[3,7,256]{2,1,0:T(8,128)} %taps_at.1, f32[16,256]{1,0:T(8,128)} %bitcast.33, ...), custom_call_target="tpu_custom_call" | custom-call | flops 8000000 | bytes 2000000 | tf_op jit(solution)/shard_map/local/pallas_call | solution.py:169
  26.3 4.8 %all-gather = f32[32,256]{1,0:T(8,128)S(1)} all-gather(f32[16,256]{1,0:T(8,128)} %get-tuple-element.16), channel_id=2, replica_groups=mesh['z'=8,'c'=2,'x'=4,'y'=8] {'c'}, dimensions={0}, use_global_device_ids=true | all-gather | bytes 49152 | tf_op jit(solution)/shard_map/all_gather | solution.py:184
  31.1 0.7 fusion.2
  31.8 22.5 %all_to_all.21.everyone = f32[8,16,256]{2,1,0:T(8,128)S(1)} all-to-all(f32[8,16,256]{2,1,0:T(8,128)S(1)} %broadcast_in_dim.13), channel_id=1, replica_groups=mesh['z'=8,'c'=2,'x'=4,'y'=8] {'z'}, dimensions={0} | all-to-all | bytes 262144 | tf_op jit(solution)/shard_map/all_to_all | solution.py:186
  54.3 0.0 copy-start
  54.3 0.9 copy-done
  55.3 0.0 copy-start.1
  55.3 0.9 copy-done.1
  56.2 0.0 copy-start.2
  56.2 0.9 copy-done.2
  57.1 0.0 copy-start.3
  57.1 0.9 copy-done.3
  58.0 0.0 copy-start.4
  58.0 0.8 copy-done.4
  58.8 1.2 join.1
  60.0 35.4 %all_to_all.22.gated = bf16[32,64,256]{2,1,0:T(8,128)(2,1)} all-to-all(bf16[32,64,256]{2,1,0:T(8,128)(2,1)S(1)} %bitcast.28), channel_id=1, replica_groups=mesh['z'=8,'c'=2,'x'=4,'y'=8] {'x','y'}, dimensions={0} | all-to-all | bytes 2097152 | tf_op jit(solution)/shard_map/all_to_all | solution.py:203
  95.4 0.0 all-gather.4.cloned.1.call-done
  95.4 6.1 %project.1 = bf16[4,256,256]{2,1,0:T(8,128)(2,1)} custom-call(bf16[32,64,256]{2,1,0:T(8,128)(2,1)} %all_to_all.22.gated, bf16[16,4,128,256]{3,2,1,0:T(8,128)(2,1)} %bitcast.30), custom_call_target="tpu_custom_call" | custom-call | flops 1073741824 | bytes 6000000 | tf_op jit(solution)/shard_map/project/pallas_call | solution.py:206
  101.5 11.5 %all_to_all.23 = bf16[4,256,256]{2,1,0:T(8,128)(2,1)S(1)} all-to-all(bf16[4,256,256]{2,1,0:T(8,128)(2,1)} %project.1), channel_id=1, replica_groups=mesh['z'=8,'c'=2,'x'=4,'y'=8] {'x'}, dimensions={0} | all-to-all | bytes 1048576 | tf_op jit(solution)/shard_map/all_to_all | solution.py:221
  113.0 0.7 fusion
  (1 shorter events, 0.0 us)
Async XLA Ops:
  6.5 88.9 %all-gather.4.cloned.1.call-start = ((), (), s32[]{:S(2)}) async-start(), calls=%async_computation.4 | async-start | bytes 4456448 | tf_op jit(solution)/shard_map/all_gather | solution.py:154
  19.1 2.1 %collective-permute-start = (bf16[3,8,256]{2,1,0:T(8,128)(2,1)S(1)}, bf16[3,8,256]{2,1,0:T(8,128)(2,1)S(1)}, u32[]{:S(2)}, u32[]{:S(2)}) collective-permute-start(bf16[3,8,256]{2,1,0:T(8,128)(2,1)S(1)} %slice.24), channel_id=1, source_target_pairs={{0,32},{32,64},{64,96},{96,128},{128,160},{160,192},{192,224},{224... | collective-permute-start | bytes 36872 | tf_op jit(solution)/shard_map/ppermute | solution.py:156
  21.2 0.6 copy-start.5
  54.3 1.0 copy-start
  55.3 0.9 copy-start.1
  56.2 0.9 copy-start.2
  57.1 0.9 copy-start.3
  58.0 0.8 copy-start.4
Sparse Core Ops, SparseCore 0:
  18.5 49.9 all-gather.3

commit v4 on v3

v4 whole, which is shorter than its diff:
```python
import jax
import jax.numpy as jnp
from jax import lax
from jax.experimental import pallas as pl
from jax.experimental.pallas import tpu as pltpu
from jax.sharding import Mesh
from jax.sharding import PartitionSpec as P

STRETCH = 64
TILE = 8
RIM = 8
SHAPE = {"zl": 2, "c": 2, "x": 4, "yl": 2}
F32 = jnp.float32
BF16 = jnp.bfloat16
Z = ("zh", "zl")
CTX = ("zh", "zl", "c")
CH = ("x", "yh", "yl")
VMEM = pl.BlockSpec(memory_space=pltpu.VMEM)
SMEM = pl.BlockSpec(memory_space=pltpu.SMEM)


def local_kernel(features, table, rim, query, inner, before, decays, slope, totals, extended, product):
    streams, rows, chans = features.shape
    stretches, modes, _ = before.shape
    width = RIM - 1
    rates = table[0:modes, :]
    gain = table[modes : 2 * modes, :]
    first = 2 * modes
    through = table[first + width : first + RIM, :]
    for k in range(stretches + 1):
        decays[k] = jnp.exp(-rates * (k * STRETCH))
    decays[stretches + 1] = jnp.exp(-rates * TILE)
    lags = lax.broadcasted_iota(jnp.int32, (TILE, chans), 0).astype(F32) + 1.0
    for n in range(modes):
        slope[n] = gain[n : n + 1, :] * jnp.exp(-rates[n : n + 1, :] * lags)
    piece = 32
    for f in range(streams):
        extended[f, 0:RIM, :] = rim[f].astype(F32)
        extended[f, RIM : RIM + rows, :] = features[f].astype(F32)
    for start in range(0, rows, piece):
        parts = []
        for f in range(streams):
            total = jnp.zeros((piece, chans), F32)
            for offset in range(width):
                at = RIM + start - offset
                tap = first + f * RIM + offset
                total = total + table[tap : tap + 1, :] * extended[f, at : at + piece, :]
            parts.append(total.astype(BF16))
        query[start : start + piece, :] = parts[0]
        product[start : start + piece, :] = (
            (parts[1].astype(F32) * parts[2].astype(F32)).astype(BF16).astype(F32)
        )
    decay = jnp.exp(-rates)

    def eight(i, states):
        states = list(states)
        base = pl.multiple_of(i * TILE, TILE)
        for k in range(stretches):
            at = pl.multiple_of(k * STRETCH + base, TILE)
            tile = product[pl.ds(at, TILE), :]
            outs = []
            state = states[k]
            for r in range(TILE):
                state = decay * state + jnp.broadcast_to(tile[r : r + 1, :], (modes, chans))
                outs.append(jnp.sum(gain * state, axis=0, keepdims=True))
            states[k] = state
            inner[pl.ds(at, TILE), :] = jnp.concatenate(outs, axis=0) + through * tile
        return tuple(states)

    zero = jnp.zeros((modes, chans), F32)
    states = lax.fori_loop(0, STRETCH // TILE, eight, (zero,) * stretches)
    across = decays[1]
    running = zero
    for k in range(stretches):
        before[k] = running
        running = across * running + states[k]
    totals[...] = running


def join_kernel(place, everyone, pair, before, decays, slope, inner, query, out, starts, gated, table):
    chips, modes, chans = everyone.shape
    stretches = before.shape[0]
    span = decays[stretches]
    chip_span = span * span
    incoming = jnp.zeros((modes, chans), F32)
    for i in range(chips):
        incoming = jnp.where(i < place[0], chip_span * incoming + everyone[i], incoming)
    incoming = jnp.where(place[1] > 0, span * incoming + pair[0], incoming)
    for k in range(stretches):
        starts[k] = decays[k] * incoming + before[k]
    table[...] = slope[...]

    def eight(i, carry):
        base = pl.multiple_of(i * TILE, TILE)
        totals = [inner[pl.ds(pl.multiple_of(k * STRETCH + base, TILE), TILE), :] for k in range(stretches)]
        for n in range(modes):
            weight = table[n]
            table[n] = weight * decays[stretches + 1, n : n + 1, :]
            for k in range(stretches):
                totals[k] = totals[k] + weight * starts[k, n : n + 1, :]
        for k in range(stretches):
            at = pl.multiple_of(k * STRETCH + base, TILE)
            gated[pl.ds(at, TILE), :] = query[pl.ds(at, TILE), :].astype(F32) * totals[k]
        return carry

    lax.fori_loop(0, STRETCH // TILE, eight, 0)
    turned = gated[...].T.astype(BF16)
    for copy in range(out.shape[0]):
        out[copy] = turned


def project_kernel(place, own, other, parts, out, weight):
    core = place[1]
    zh, zl, blocks, height, half = parts.shape
    depth = zh * height
    for b in range(blocks):
        block = jnp.where(core == b, 0, 1)
        for i in range(zh):
            for l in range(zl):
                weight[i * height : (i + 1) * height, l * half : (l + 1) * half] = parts[i, l, block]
        right = weight[...]
        for left, core_of in ((own, core), (other, 1 - core)):
            left = left[...].reshape(depth, left.shape[2])
            total = lax.dot_general(left, right, (((0,), (0,)), ((), ())), preferred_element_type=F32)
            total = total.astype(BF16)
            for l in range(zl):
                out[(b * zl + l) * 2 + core_of] = total[:, l * half : (l + 1) * half]


def finish_kernel(shares, out):
    halves = 2
    half = shares.shape[2]
    for h in range(halves):
        total = shares[h].astype(F32)
        for i in range(1, shares.shape[0] // halves):
            total = total + shares[i * halves + h].astype(F32)
        out[:, h * half : (h + 1) * half] = total.astype(BF16)


def cost(flops, moved):
    return pl.CostEstimate(flops=flops, bytes_accessed=moved, transcendentals=0)


def per_device(features, short_weight, rates, residues, skip, out_weight):
    streams, rows, chans = features.shape
    modes = rates.shape[1]
    width = short_weight.shape[1]
    zh, zl, xs = lax.axis_size("zh"), lax.axis_size("zl"), lax.axis_size("x")
    yh, yl = lax.axis_size("yh"), lax.axis_size("yl")
    length = lax.axis_size(CTX)
    high = lax.axis_index("yh") // zl
    place = jnp.stack([lax.axis_index(Z), lax.axis_index("c")]).astype(jnp.int32)
    shape = jax.ShapeDtypeStruct
    limit = pltpu.CompilerParams(vmem_limit_bytes=32 << 20)

    deep, wide = out_weight.shape
    half = wide // 2
    low_half, high_half = out_weight[:, :half], out_weight[:, half:]
    routes = []
    for flip in (0, 1):
        pairs = []
        for q in range(zl * 2):
            for n in range(yh):
                core = (n // zl) ^ flip
                pairs.append((q * yh + n, ((n % zl) * 2 + core) * yh + q))
        value = jnp.where((high ^ flip) == 0, low_half, high_half)
        routes.append(lax.ppermute(value, ("zl", "c", "yh"), pairs))
    sliced = jnp.stack(routes)

    rim = lax.ppermute(features[:, rows - RIM :, :], CTX, [(i, i + 1) for i in range(length - 1)])
    blank = jnp.zeros((1, chans), F32)
    rest = [short_weight[0], skip[None, :]]
    for f in range(1, streams):
        rest += [short_weight[f], blank]
    table = jnp.concatenate([rates.T, residues.T] + rest, axis=0)
    rim, table, place = lax.optimization_barrier((rim, table, place))

    stretches = rows // STRETCH
    shapes = (
        shape((rows, chans), BF16),
        shape((rows, chans), F32),
        shape((stretches, modes, chans), F32),
        shape((stretches + 2, modes, chans), F32),
        shape((modes, TILE, chans), F32),
        shape((modes, chans), F32),
    )
    query, inner, before, decays, slope, totals = pl.pallas_call(
        local_kernel,
        out_shape=shapes,
        in_specs=[VMEM] * 3,
        out_specs=(VMEM,) * len(shapes),
        scratch_shapes=[pltpu.VMEM((streams, rows + RIM, chans), F32), pltpu.VMEM((rows, chans), F32)],
        cost_estimate=cost(8_000_000, 2_000_000),
        compiler_params=limit,
        name="local",
    )(features, table, rim)
    pair = lax.all_gather(totals, "c", axis=0, tiled=False)
    chip = decays[stretches] * pair[0] + pair[1]
    chip, sliced = lax.optimization_barrier((chip, sliced))
    weights = lax.all_gather(sliced, Z, axis=0, tiled=False)
    everyone = lax.all_to_all(
        jnp.broadcast_to(chip[None], (zh * zl, modes, chans)), Z, split_axis=0, concat_axis=0, tiled=True
    )
    spread = pl.pallas_call(
        join_kernel,
        out_shape=shape((xs * yl, chans, rows), BF16),
        in_specs=[SMEM] + [VMEM] * 7,
        out_specs=VMEM,
        scratch_shapes=[
            pltpu.VMEM((stretches, modes, chans), F32),
            pltpu.VMEM((rows, chans), F32),
            pltpu.VMEM((modes, TILE, chans), F32),
        ],
        cost_estimate=cost(4_000_000, 4_000_000),
        compiler_params=limit,
        name="join",
    )(place, everyone, pair, before, decays, slope, inner, query)
    own = lax.all_to_all(spread, ("x", "yl"), split_axis=0, concat_axis=0, tiled=True)
    other = lax.ppermute(own, "c", [(0, 1), (1, 0)])
    depth = xs * yl * chans
    partial = pl.pallas_call(
        project_kernel,
        out_shape=shape((yh * 2, rows, half), BF16),
        in_specs=[SMEM, VMEM, VMEM, VMEM],
        out_specs=VMEM,
        scratch_shapes=[pltpu.VMEM((depth, zl * half), BF16)],
        cost_estimate=cost(4 * rows * depth * half * yh, 6_000_000),
        compiler_params=pltpu.CompilerParams(vmem_limit_bytes=48 << 20),
        name="project",
    )(place, own, other, weights.reshape(zh, zl, 2, deep, half))
    shares = lax.all_to_all(partial, ("yh", "c"), split_axis=0, concat_axis=0, tiled=True)
    return pl.pallas_call(
        finish_kernel,
        out_shape=shape((rows, wide), BF16),
        in_specs=[VMEM],
        out_specs=VMEM,
        cost_estimate=cost(500_000, 700_000),
        compiler_params=limit,
        name="finish",
    )(shares)


def solution(mesh):
    zl, cores, xs, yl = (SHAPE[name] for name in ("zl", "c", "x", "yl"))
    zh = mesh.shape["ctx"] // (zl * cores)
    yh = mesh.shape["ch"] // (xs * yl)
    fine = Mesh(mesh.devices.reshape(zh, zl, cores, xs, yh, yl), CTX + CH)
    return jax.shard_map(
        per_device,
        mesh=fine,
        in_specs=(
            P(None, CTX, CH),
            P(None, None, CH),
            P(CH, None),
            P(CH, None),
            P(CH),
            P(CTX, CH),
        ),
        out_specs=P(CTX, CH),
        check_vma=False,
    )
```

time: 121 us -> 113 us (0.934)
  the two profiles are of different devices: /device:TPU:8 before, /device:TPU:2 now
where the time goes in v4:
time: 113 us; the launch traced here: 112 us
  blocking collectives  69 us (61%)
  between operations  13.5 us (12%)
  starting transfers between devices  10.2 us (9%)
  local copies, waits for them, and re-layouts  6.22 us (6%)
  waiting for transfers between devices  6 us (5%)
  Pallas kernels  5.78 us (5%)
  other arithmetic  1.79 us (2%)
    all_to_all x1, blocking collectives, per_device(): lax.all_to_all(partial, ('yh', 'c'), split_axis=0, concat_axis=0, tiled=T...  24.1 us
    all_to_all x1, blocking collectives, per_device(): lax.all_to_all(jnp.broadcast_to(chip[None], (zh * zl, modes, chans)), Z,...  23 us
    all_to_all x1, blocking collectives, per_device(): lax.all_to_all(spread, ('x', 'yl'), split_axis=0, concat_axis=0, tiled=True)  18.2 us
    ppermute x2, starting transfers between devices, per_device(): routes.append(lax.ppermute(value, ('zl', 'c', 'yh'), pairs))  6.52 us
    all_gather x1, blocking collectives, per_device(): pair = lax.all_gather(totals, 'c', axis=0, tiled=False)  3.75 us
    all_gather x1, waiting for transfers between devices, per_device(): weights = lax.all_gather(sliced, Z, axis=0, tiled=False)  3.35 us
    ppermute x1, waiting for transfers between devices, per_device(): other = lax.ppermute(own, 'c', [(0, 1), (1, 0)])  2.63 us
    unnamed x4, local copies, waits for them, and re-layouts  2.59 us
  transfers between devices with their start and end apart: 5, of which 2 were waited for; matrix products, arithmetic and copies ran while one was open for 4% of the time, Pallas kernels for 3%

profile of v4, /device:TPU:2, one launch (start us, length us, event | category | flops | bytes accessed | tf_op | source)
XLA Modules:
  0.0 112.5 jit_solution(12470705876699197019)
XLA Ops:
  6.5 0.0 all-gather.4.cloned.1.call-start
  6.5 0.7 slice.27
  7.3 1.7 %collective-permute-start = (bf16[3,8,256]{2,1,0:T(8,128)(2,1)S(1)}, bf16[3,8,256]{2,1,0:T(8,128)(2,1)S(1)}, u32[]{:S(2)}, u32[]{:S(2)}) collective-permute-start(bf16[3,8,256]{2,1,0:T(8,128)(2,1)S(1)} %slice.27), channel_id=1, source_target_pairs={{0,32},{32,64},{64,96},{96,128},{128,160},{160,192},{192,224},{224... | collective-permute-start | bytes 36872 | tf_op jit(solution)/shard_map/ppermute | solution.py:170
  9.0 1.0 broadcast_select_fusion.1
  10.0 0.7 collective-permute-start.1
  10.7 5.9 %collective-permute-start.2 = (bf16[512,128]{1,0:T(8,128)(2,1)S(1)}, bf16[512,128]{1,0:T(8,128)(2,1)S(1)}, u32[]{:S(2)}, u32[]{:S(2)}) collective-permute-start(bf16[512,128]{1,0:T(8,128)(2,1)S(1)} %get-tuple-element.28), channel_id=1, source_target_pairs={{0,32},{2,96},{4,0},{6,64},{32,34},{34,98},{36,2},{38,66},{64,36},... | collective-permute-start | bytes 393224 | tf_op jit(solution)/shard_map/ppermute | solution.py:167
  16.5 0.7 slice_bitcast_fusion.2
  17.3 0.1 pad_add_fusion.place
  17.4 2.2 %concatenate.3.table = f32[56,256]{1,0:T(8,128)S(1)} concatenate(f32[16,256]{1,0:T(8,128)} %bitcast.33, f32[16,256]{1,0:T(8,128)} %bitcast.34, f32[7,256]{1,0:T(8,128)S(1)} %get-tuple-element.30, f32[1,256]{1,0:T(1,128)} %bitcast.35, f32[7,256]{1,0:T(8,128)S(1)} %get-tuple-element.31, f32[1,256]{1,0:T(1,128)S(1)} %broadcast_in_dim.13, f32[7,256]{1,0:T(8,128)S(1)} %get-tuple-element.29, ...), dimensions={0} | concatenate | bytes 114688 | tf_op jit(solution)/shard_map/concatenate | solution.py:175
  19.5 0.0 collective-permute-done.rim
  19.5 0.0 copy-start.1
  19.5 1.0 copy-done.1
  20.5 1.9 %local.1 = (bf16[256,256]{1,0:T(8,128)(2,1)S(1)}, f32[256,256]{1,0:T(8,128)S(1)}, f32[4,16,256]{2,1,0:T(8,128)S(1)}, f32[6,16,256]{2,1,0:T(8,128)S(1)}, f32[16,8...) custom-call(bf16[3,256,256]{2,1,0:T(8,128)(2,1)S(1)} %copy-done.1, f32[56,256]{1,0:T(8,128)S(1)} %concatenate.3.table, ...), custom_call_target="tpu_custom_call" | custom-call | flops 8000000 | bytes 2000000 | tf_op jit(solution)/shard_map/local/pallas_call | solution.py:187
  22.4 3.8 %all-gather = f32[32,256]{1,0:T(8,128)S(1)} all-gather(f32[16,256]{1,0:T(8,128)S(1)} %get-tuple-element.20), channel_id=2, replica_groups=mesh['zh'=4,'zl'=2,'c'=2,'x'=4,'yh'=4,'yl'=2] {'c'}, dimensions={0}, use_global_device_ids=true | all-gather | bytes 49152 | tf_op jit(solution)/shard_map/all_gather | solution.py:197
  26.2 0.0 collective-permute-done.1
  26.2 0.0 collective-permute-done.2
  26.2 0.7 pad_maximum_fusion
  26.9 0.0 all-gather.4.cloned.1.call-update
  27.0 23.0 %all_to_all.15.everyone = f32[8,16,256]{2,1,0:T(8,128)S(1)} all-to-all(f32[8,16,256]{2,1,0:T(8,128)S(1)} %broadcast_in_dim.14), channel_id=1, replica_groups=mesh['zh'=4,'zl'=2,'c'=2,'x'=4,'yh'=4,'yl'=2] {'zh','zl'}, dimensions={0} | all-to-all | bytes 262144 | tf_op jit(solution)/shard_map/all_to_all | solution.py:201
  49.9 1.2 %join.1 = bf16[8,256,256]{2,1,0:T(8,128)(2,1)S(1)} custom-call(s32[2]{0:T(128)S(1)} %pad_add_fusion.place, f32[8,16,256]{2,1,0:T(8,128)S(1)} %all_to_all.15.everyone, f32[2,16,256]{2,1,0:T(8,128)S(1)} %bitcast.30, f32[4,16,256]{2,1,0:T(8,128)S(1)} %get-tuple-element.22.before, f32[6,16,256]{2,1,0:T(8,128)S(1)} %get-tuple-element.19.decays, ...), custom_call_target="tpu_custom_call" | custom-call | flops 4000000 | bytes 4000000 | tf_op jit(solution)/shard_map/join/pallas_call | solution.py:204
  51.1 18.2 %all_to_all.16.own = bf16[8,256,256]{2,1,0:T(8,128)(2,1)S(1)} all-to-all(bf16[8,256,256]{2,1,0:T(8,128)(2,1)S(1)} %join.1), channel_id=1, replica_groups=mesh['zh'=4,'zl'=2,'c'=2,'x'=4,'yh'=4,'yl'=2] {'x','yl'}, dimensions={0} | all-to-all | bytes 2097152 | tf_op jit(solution)/shard_map/all_to_all | solution.py:218
  69.3 1.9 %collective-permute-start.3 = (bf16[8,256,256]{2,1,0:T(8,128)(2,1)S(1)}, bf16[8,256,256]{2,1,0:T(8,128)(2,1)S(1)}, u32[]{:S(2)}, u32[]{:S(2)}) collective-permute-start(bf16[8,256,256]{2,1,0:T(8,128)(2,1)S(1)} %all_to_all.16.own), channel_id=1, source_target_pairs={{0,32},{32,0},{1,33},{33,1},{2,34},{34,2},{3,35},{35,3},{4,36},{36... | collective-permute-start | bytes 3145736 | tf_op jit(solution)/shard_map/ppermute | solution.py:219
  71.2 2.6 %collective-permute-done.3.other = bf16[8,256,256]{2,1,0:T(8,128)(2,1)S(1)} collective-permute-done((bf16[8,256,256]{2,1,0:T(8,128)(2,1)S(1)}, bf16[8,256,256]{2,1,0:T(8,128)(2,1)S(1)}, u32[]{:S(2)}, u32[]{:S(2)}) %collective-permute-start.3) | collective-permute-done | bytes 1048608 | tf_op jit(solution)/shard_map/ppermute | solution.py:219
  73.8 3.3 %all-gather.4.cloned.1.call-done = bf16[16,512,128]{2,1,0:T(8,128)(2,1)} async-done(((bf16[2,512,128]{2,1,0:T(8,128)(2,1)}), bf16[16,512,128]{2,1,0:T(8,128)(2,1)}) %all-gather.4.cloned.1.call-update) | async-done | bytes 2097168 | tf_op jit(solution)/shard_map/all_gather | solution.py:200
  77.2 0.0 copy-start
  77.2 1.6 %copy-done = bf16[16,512,128]{2,1,0:T(8,128)(2,1)S(1)} copy-done((bf16[16,512,128]{2,1,0:T(8,128)(2,1)S(1)}, bf16[16,512,128]{2,1,0:T(8,128)(2,1)}, u32[]{:S(2)}) %copy-start) | copy-done | bytes 2097176
  78.8 2.0 %project.1 = bf16[8,256,128]{2,1,0:T(8,128)(2,1)S(1)} custom-call(s32[2]{0:T(128)S(1)} %pad_add_fusion.place, bf16[8,256,256]{2,1,0:T(8,128)(2,1)S(1)} %all_to_all.16.own, bf16[8,256,256]{2,1,0:T(8,128)(2,1)S(1)} %collective-permute-done.3.other, bf16[4,2,2,512,128]{4,3,2,1,0:T(8,128)(2,1)S(1)} %bitcast.29), custom_call_target="tpu_custom_call" | custom-call | flops 1073741824 | bytes 6000000 | tf_op jit(solution)/shard_map/project/pallas_call | solution.py:221
  80.8 24.1 %all_to_all.17.shares = bf16[8,256,128]{2,1,0:T(8,128)(2,1)S(1)} all-to-all(bf16[8,256,128]{2,1,0:T(8,128)(2,1)S(1)} %project.1), channel_id=1, replica_groups=mesh['zh'=4,'zl'=2,'c'=2,'x'=4,'yh'=4,'yl'=2] {'yh','c'}, dimensions={0} | all-to-all | bytes 1048576 | tf_op jit(solution)/shard_map/all_to_all | solution.py:231
  104.9 0.7 finish.1
  (3 shorter events, 0.0 us)
Async XLA Ops:
  6.5 70.7 %all-gather.4.cloned.1.call-start = ((), (), s32[]{:S(2)}) async-start(), calls=%async_computation.3 | async-start | bytes 2359296 | tf_op jit(solution)/shard_map/all_gather | solution.py:200
  7.3 12.3 %collective-permute-start = (bf16[3,8,256]{2,1,0:T(8,128)(2,1)S(1)}, bf16[3,8,256]{2,1,0:T(8,128)(2,1)S(1)}, u32[]{:S(2)}, u32[]{:S(2)}) collective-permute-start(bf16[3,8,256]{2,1,0:T(8,128)(2,1)S(1)} %slice.27), channel_id=1, source_target_pairs={{0,32},{32,64},{64,96},{96,128},{128,160},{160,192},{192,224},{224... | collective-permute-start | bytes 36872 | tf_op jit(solution)/shard_map/ppermute | solution.py:170
  10.0 16.2 %collective-permute-start.1 = (bf16[512,128]{1,0:T(8,128)(2,1)S(1)}, bf16[512,128]{1,0:T(8,128)(2,1)S(1)}, u32[]{:S(2)}, u32[]{:S(2)}) collective-permute-start(bf16[512,128]{1,0:T(8,128)(2,1)S(1)} %get-tuple-element.27), channel_id=1, source_target_pairs={{0,0},{2,64},{4,32},{6,96},{32,2},{34,66},{36,34},{38,98},{64,4},{... | collective-permute-start | bytes 393224 | tf_op jit(solution)/shard_map/ppermute | solution.py:167
  10.7 15.5 %collective-permute-start.2 = (bf16[512,128]{1,0:T(8,128)(2,1)S(1)}, bf16[512,128]{1,0:T(8,128)(2,1)S(1)}, u32[]{:S(2)}, u32[]{:S(2)}) collective-permute-start(bf16[512,128]{1,0:T(8,128)(2,1)S(1)} %get-tuple-element.28), channel_id=1, source_target_pairs={{0,32},{2,96},{4,0},{6,64},{32,34},{34,98},{36,2},{38,66},{64,36},... | collective-permute-start | bytes 393224 | tf_op jit(solution)/shard_map/ppermute | solution.py:167
  19.5 1.0 copy-start.1
  69.3 4.5 %collective-permute-start.3 = (bf16[8,256,256]{2,1,0:T(8,128)(2,1)S(1)}, bf16[8,256,256]{2,1,0:T(8,128)(2,1)S(1)}, u32[]{:S(2)}, u32[]{:S(2)}) collective-permute-start(bf16[8,256,256]{2,1,0:T(8,128)(2,1)S(1)} %all_to_all.16.own), channel_id=1, source_target_pairs={{0,32},{32,0},{1,33},{33,1},{2,34},{34,2},{3,35},{35,3},{4,36},{36... | collective-permute-start | bytes 3145736 | tf_op jit(solution)/shard_map/ppermute | solution.py:219
  77.2 1.6 %copy-start = (bf16[16,512,128]{2,1,0:T(8,128)(2,1)S(1)}, bf16[16,512,128]{2,1,0:T(8,128)(2,1)}, u32[]{:S(2)}) copy-start(bf16[16,512,128]{2,1,0:T(8,128)(2,1)} %all-gather.4.cloned.1.call-done) | copy-start | bytes 6291460
Sparse Core Ops, SparseCore 0:
  27.1 50.0 all-gather.3

commit v5 on v3

--- a/solution.py
+++ b/solution.py
@@ -21,26 +21,28 @@
 
 def local_kernel(
     features_at, taps_at, rates_at, gains_at, skip_at, rim, query, inner, before, decays, slope, totals,
-    features, taps, rates, gains, skip, sems, extended, product,
+    features, taps, rates_in, gains_in, skip, sems, extended, product,
 ):
-    pairs = ((rates_at, rates), (gains_at, gains), (features_at, features), (taps_at, taps), (skip_at, skip))
+    pairs = ((rates_at, rates_in), (gains_at, gains_in), (features_at, features), (taps_at, taps), (skip_at, skip))
     copies = [pltpu.make_async_copy(src, dst, sems.at[i]) for i, (src, dst) in enumerate(pairs)]
     for copy in copies:
         copy.start()
     streams, rows, chans = features.shape
+    stretches, modes, _ = before.shape
     width = taps.shape[1]
-    modes = rates.shape[0]
-    stretches = rows // STRETCH
     for copy in copies[:2]:
         copy.wait()
+    rates = rates_in[...]
+    gain = gains_in[...]
     for k in range(stretches + 1):
-        decays[k] = jnp.exp(-rates[...] * (k * STRETCH))
-    decays[stretches + 1] = jnp.exp(-rates[...] * TILE)
+        decays[k] = jnp.exp(-rates * (k * STRETCH))
+    decays[stretches + 1] = jnp.exp(-rates * TILE)
     lags = lax.broadcasted_iota(jnp.int32, (TILE, chans), 0).astype(F32) + 1.0
     for n in range(modes):
-        slope[n] = gains[n : n + 1, :] * jnp.exp(-rates[n : n + 1, :] * lags)
+        slope[n] = gain[n : n + 1, :] * jnp.exp(-rates[n : n + 1, :] * lags)
     for copy in copies[2:]:
         copy.wait()
+    through = skip[...]
     piece = 32
     for f in range(streams):
         extended[f, 0:RIM, :] = rim[f].astype(F32)
@@ -57,27 +59,25 @@
         product[start : start + piece, :] = (
             (parts[1].astype(F32) * parts[2].astype(F32)).astype(BF16).astype(F32)
         )
-    decay = jnp.exp(-rates[...])
-    gain = gains[...]
-    through = skip[...]
+    decay = jnp.exp(-rates)
 
     def eight(i, states):
         states = list(states)
-        base = pl.multiple_of(i * 8, 8)
+        base = pl.multiple_of(i * TILE, TILE)
         for k in range(stretches):
-            at = pl.multiple_of(k * STRETCH + base, 8)
-            tile = product[pl.ds(at, 8), :]
+            at = pl.multiple_of(k * STRETCH + base, TILE)
+            tile = product[pl.ds(at, TILE), :]
             outs = []
             state = states[k]
-            for r in range(8):
+            for r in range(TILE):
                 state = decay * state + jnp.broadcast_to(tile[r : r + 1, :], (modes, chans))
                 outs.append(jnp.sum(gain * state, axis=0, keepdims=True))
             states[k] = state
-            inner[pl.ds(at, 8), :] = jnp.concatenate(outs, axis=0) + through * tile
+            inner[pl.ds(at, TILE), :] = jnp.concatenate(outs, axis=0) + through * tile
         return tuple(states)
 
     zero = jnp.zeros((modes, chans), F32)
-    states = lax.fori_loop(0, STRETCH // 8, eight, (zero,) * stretches)
+    states = lax.fori_loop(0, STRETCH // TILE, eight, (zero,) * stretches)
     across = decays[1]
     running = zero
     for k in range(stretches):
@@ -97,28 +97,26 @@
     incoming = jnp.where(place[1] > 0, span * incoming + pair[0], incoming)
     for k in range(stretches):
         starts[k] = decays[k] * incoming + before[k]
-
     table[...] = slope[...]
 
     def eight(i, carry):
-        base = pl.multiple_of(i * 8, 8)
-        totals = [inner[pl.ds(pl.multiple_of(k * STRETCH + base, 8), 8), :] for k in range(stretches)]
+        base = pl.multiple_of(i * TILE, TILE)
+        totals = [inner[pl.ds(pl.multiple_of(k * STRETCH + base, TILE), TILE), :] for k in range(stretches)]
         for n in range(modes):
             weight = table[n]
             table[n] = weight * decays[stretches + 1, n : n + 1, :]
             for k in range(stretches):
                 totals[k] = totals[k] + weight * starts[k, n : n + 1, :]
         for k in range(stretches):
-            at = pl.multiple_of(k * STRETCH + base, 8)
-            gated[pl.ds(at, 8), :] = query[pl.ds(at, 8), :].astype(F32) * totals[k]
+            at = pl.multiple_of(k * STRETCH + base, TILE)
+            gated[pl.ds(at, TILE), :] = query[pl.ds(at, TILE), :].astype(F32) * totals[k]
         return carry
 
-    lax.fori_loop(0, STRETCH // 8, eight, 0)
+    lax.fori_loop(0, STRETCH // TILE, eight, 0)
     turned = gated[...].T.astype(BF16)
-    blocks = out.shape[0]
-    height = out.shape[2]
+    blocks, copies, height, _ = out.shape
     for b in range(blocks):
-        for copy in range(out.shape[1]):
+        for copy in range(copies):
             out[b, copy] = turned[b * height : (b + 1) * height, :]
 
 
@@ -128,11 +126,12 @@
     for copy in copies:
         copy.start()
     depth = gated.shape[0] * gated.shape[1]
-    left = gated[...].reshape(depth, gated.shape[2]).T
+    left = gated[...].reshape(depth, gated.shape[2])
     for i in range(parts):
         copies[i].wait()
         right = weight[i].reshape(depth, weight.shape[3])
-        out[i] = jnp.dot(left, right, preferred_element_type=F32).astype(BF16)
+        total = lax.dot_general(left, right, (((0,), (0,)), ((), ())), preferred_element_type=F32)
+        out[i] = total.astype(BF16)
 
 
 def mixed_of(features, short_weight, rates, residues, skip, out_weight):
@@ -166,10 +165,11 @@
         shape((modes, chans), F32),
     )
     operands = (features, short_weight, decay_rate, mode_gain, skip[None, :])
+    operands = tuple(pltpu.with_memory_space_constraint(v, pltpu.HBM) for v in operands)
     query, inner, before, decays, slope, totals = pl.pallas_call(
         local_kernel,
         out_shape=shapes,
-        in_specs=[pl.BlockSpec(memory_space=pl.ANY)] * len(operands) + [VMEM],
+        in_specs=[pl.BlockSpec(memory_space=pltpu.HBM)] * len(operands) + [VMEM],
         out_specs=(VMEM,) * len(shapes),
         scratch_shapes=[pltpu.VMEM(v.shape, v.dtype) for v in operands]
         + [
@@ -178,7 +178,7 @@
             pltpu.VMEM((rows, chans), F32),
         ],
         cost_estimate=pl.CostEstimate(flops=8_000_000, bytes_accessed=2_000_000, transcendentals=0),
-        compiler_params=pltpu.CompilerParams(vmem_limit_bytes=60 << 20),
+        compiler_params=pltpu.CompilerParams(vmem_limit_bytes=32 << 20),
         name="local",
     )(*operands, rim)
     pair = lax.all_gather(totals, "c", axis=0, tiled=False)
@@ -203,19 +203,17 @@
     gathered = lax.all_to_all(
         spread.reshape(xs * ys, piece, rows), CH, split_axis=0, concat_axis=0, tiled=True
     )
+    weights = pltpu.with_memory_space_constraint(weights.reshape(length, xs, height, wide), pltpu.HBM)
     partial = pl.pallas_call(
         project_kernel,
         out_shape=shape((xs, rows, wide), BF16),
         in_specs=[VMEM, pl.BlockSpec(memory_space=pl.ANY)],
         out_specs=VMEM,
-        scratch_shapes=[
-            pltpu.VMEM((xs, length, height, wide), BF16),
-            pltpu.SemaphoreType.DMA((xs,)),
-        ],
+        scratch_shapes=[pltpu.VMEM((xs, length, height, wide), BF16), pltpu.SemaphoreType.DMA((xs,))],
         cost_estimate=pl.CostEstimate(
-            flops=2 * rows * length * height * wide * xs, bytes_accessed=6_000_000, transcendentals=0
+            flops=2 * rows * xs * ys * piece * wide * xs, bytes_accessed=6_000_000, transcendentals=0
         ),
-        compiler_params=pltpu.CompilerParams(vmem_limit_bytes=58 << 20),
+        compiler_params=pltpu.CompilerParams(vmem_limit_bytes=32 << 20),
         name="project",
     )(gathered, weights)
     shares = lax.all_to_all(partial, "x", split_axis=0, concat_axis=0, tiled=True)

time: 121 us -> 111 us (0.917)
  local copies, waits for them, and re-layouts: 6.78 us -> 1.7 us
  Pallas kernels: 11.7 us -> 8.16 us
    unnamed x12 -> x0, local copies, waits for them, and re-layouts: 5.09 us -> none
    pallas_call x1, Pallas kernels: 6.09 us -> 4.04 us  [mixed_of(): pl.pallas_call(project_kernel, out_shape=shape((xs, rows, wide), BF16), i...]
    pallas_call x1, Pallas kernels: 4.43 us -> 2.94 us  [mixed_of(): pl.pallas_call(local_kernel, out_shape=shapes, in_specs=[pl.BlockSpec(mem...]
  transfers between devices with their start and end apart: 2 -> 2, of which waited for: 1 -> 1; matrix products, arithmetic and copies ran while one was open for 1% -> 1% of each run, Pallas kernels for 5% -> 4%
where the time goes in v5:
time: 111 us
  blocking collectives  84.5 us (76%)
  between operations  13.4 us (12%)
  Pallas kernels  8.16 us (7%)
  local copies, waits for them, and re-layouts  1.7 us (2%)
  starting transfers between devices  1.28 us (1%)
    all_to_all x1, blocking collectives, mixed_of(): lax.all_to_all(spread.reshape(xs * ys, piece, rows), CH, split_axis=0, co...  35.8 us
    all_to_all x1, blocking collectives, mixed_of(): lax.all_to_all(jnp.broadcast_to(chip[None], (zs, modes, chans)), 'z', spl...  22.5 us
    all_to_all x1, blocking collectives, mixed_of(): lax.all_to_all(sliced, 'x', split_axis=0, concat_axis=0, tiled=True)  10.9 us
    all_to_all x1, blocking collectives, mixed_of(): lax.all_to_all(partial, 'x', split_axis=0, concat_axis=0, tiled=True)  10.7 us
    all_gather x1, blocking collectives, mixed_of(): pair = lax.all_gather(totals, 'c', axis=0, tiled=False)  4.58 us
    pallas_call x1, Pallas kernels, mixed_of(): pl.pallas_call(project_kernel, out_shape=shape((xs, rows, wide), BF16), i...  4.04 us
    pallas_call x1, Pallas kernels, mixed_of(): pl.pallas_call(local_kernel, out_shape=shapes, in_specs=[pl.BlockSpec(mem...  2.94 us
  transfers between devices with their start and end apart: 2, of which 1 were waited for; matrix products, arithmetic and copies ran while one was open for 1% of the time, Pallas kernels for 4%

profile of v5, /device:TPU:8, one launch (start us, length us, event | category | flops | bytes accessed | tf_op | source)
XLA Modules:
  0.0 110.7 jit_solution(6011287030147190699)
XLA Ops:
  6.5 0.0 all-gather.4.cloned.1.call-start
  6.5 1.0 copy.8
  7.5 10.9 %all_to_all.20 = bf16[4,128,256]{2,1,0:T(8,128)(2,1)} all-to-all(bf16[4,128,256]{2,1,0:T(8,128)(2,1)S(1)} %bitcast.31), channel_id=1, replica_groups=mesh['z'=8,'c'=2,'x'=4,'y'=8] {'x'}, dimensions={0} | all-to-all | bytes 524288 | tf_op jit(solution)/shard_map/all_to_all | solution.py:152
  18.4 0.0 all-gather.4.cloned.1.call-update
  18.4 0.7 slice.24
  19.1 1.3 %collective-permute-start = (bf16[3,8,256]{2,1,0:T(8,128)(2,1)S(1)}, bf16[3,8,256]{2,1,0:T(8,128)(2,1)S(1)}, u32[]{:S(2)}, u32[]{:S(2)}) collective-permute-start(bf16[3,8,256]{2,1,0:T(8,128)(2,1)S(1)} %slice.24), channel_id=1, source_target_pairs={{0,32},{32,64},{64,96},{96,128},{128,160},{160,192},{192,224},{224... | collective-permute-start | bytes 36872 | tf_op jit(solution)/shard_map/ppermute | solution.py:155
  20.4 0.1 pad_add_fusion.place
  20.5 0.7 collective-permute-done.rim
  21.2 2.9 %local.1 = (bf16[256,256]{1,0:T(8,128)(2,1)S(1)}, f32[256,256]{1,0:T(8,128)S(1)}, f32[4,16,256]{2,1,0:T(8,128)S(1)}, f32[6,16,256]{2,1,0:T(8,128)S(1)}, f32[16,8...) custom-call(bf16[3,256,256]{2,1,0:T(8,128)(2,1)} %features_at.1, f32[3,7,256]{2,1,0:T(8,128)} %taps_at.1, f32[16,256]{1,0:T(8,128)} %bitcast.33, ...), custom_call_target="tpu_custom_call" | custom-call | flops 8000000 | bytes 2000000 | tf_op jit(solution)/shard_map/local/pallas_call | solution.py:169
  24.2 4.6 %all-gather = f32[32,256]{1,0:T(8,128)S(1)} all-gather(f32[16,256]{1,0:T(8,128)S(1)} %get-tuple-element.16), channel_id=2, replica_groups=mesh['z'=8,'c'=2,'x'=4,'y'=8] {'c'}, dimensions={0}, use_global_device_ids=true | all-gather | bytes 49152 | tf_op jit(solution)/shard_map/all_gather | solution.py:184
  28.8 22.5 %all_to_all.21.everyone = f32[8,16,256]{2,1,0:T(8,128)S(1)} all-to-all(f32[8,16,256]{2,1,0:T(8,128)S(1)} %broadcast_in_dim.13), channel_id=1, replica_groups=mesh['z'=8,'c'=2,'x'=4,'y'=8] {'z'}, dimensions={0} | all-to-all | bytes 262144 | tf_op jit(solution)/shard_map/all_to_all | solution.py:186
  51.3 1.2 %join.1 = bf16[4,8,64,256]{3,2,1,0:T(8,128)(2,1)S(1)} custom-call(s32[2]{0:T(128)S(1)} %pad_add_fusion.place, f32[8,16,256]{2,1,0:T(8,128)S(1)} %all_to_all.21.everyone, f32[2,16,256]{2,1,0:T(8,128)S(1)} %bitcast.29, f32[4,16,256]{2,1,0:T(8,128)S(1)} %get-tuple-element.17.before, f32[6,16,256]{2,1,0:T(8,128)S(1)} %get-tuple-element.15.decays, ...), custom_call_target="tpu_custom_call" | custom-call | flops 4000000 | bytes 4000000 | tf_op jit(solution)/shard_map/join/pallas_call | solution.py:189
  52.5 35.8 %all_to_all.22.gated = bf16[32,64,256]{2,1,0:T(8,128)(2,1)S(1)} all-to-all(bf16[32,64,256]{2,1,0:T(8,128)(2,1)S(1)} %bitcast.28), channel_id=1, replica_groups=mesh['z'=8,'c'=2,'x'=4,'y'=8] {'x','y'}, dimensions={0} | all-to-all | bytes 2097152 | tf_op jit(solution)/shard_map/all_to_all | solution.py:203
  88.3 0.0 all-gather.4.cloned.1.call-done
  88.3 4.0 %project.1 = bf16[4,256,256]{2,1,0:T(8,128)(2,1)S(1)} custom-call(bf16[32,64,256]{2,1,0:T(8,128)(2,1)S(1)} %all_to_all.22.gated, bf16[16,4,128,256]{3,2,1,0:T(8,128)(2,1)} %bitcast.30), custom_call_target="tpu_custom_call" | custom-call | flops 1073741824 | bytes 6000000 | tf_op jit(solution)/shard_map/project/pallas_call | solution.py:207
  92.4 10.7 %all_to_all.23 = bf16[4,256,256]{2,1,0:T(8,128)(2,1)S(1)} all-to-all(bf16[4,256,256]{2,1,0:T(8,128)(2,1)S(1)} %project.1), channel_id=1, replica_groups=mesh['z'=8,'c'=2,'x'=4,'y'=8] {'x'}, dimensions={0} | all-to-all | bytes 1048576 | tf_op jit(solution)/shard_map/all_to_all | solution.py:219
  103.1 0.7 fusion
  (2 shorter events, 0.0 us)
Async XLA Ops:
  6.5 81.8 %all-gather.4.cloned.1.call-start = ((), (), s32[]{:S(2)}) async-start(), calls=%async_computation.4 | async-start | bytes 4456448 | tf_op jit(solution)/shard_map/all_gather | solution.py:153
  19.1 2.1 %collective-permute-start = (bf16[3,8,256]{2,1,0:T(8,128)(2,1)S(1)}, bf16[3,8,256]{2,1,0:T(8,128)(2,1)S(1)}, u32[]{:S(2)}, u32[]{:S(2)}) collective-permute-start(bf16[3,8,256]{2,1,0:T(8,128)(2,1)S(1)} %slice.24), channel_id=1, source_target_pairs={{0,32},{32,64},{64,96},{96,128},{128,160},{160,192},{192,224},{224... | collective-permute-start | bytes 36872 | tf_op jit(solution)/shard_map/ppermute | solution.py:155
Sparse Core Ops, SparseCore 0:
  18.5 50.0 all-gather.3

commit v6 on v5

--- a/solution.py
+++ b/solution.py
@@ -10,11 +10,12 @@
 STRETCH = 64
 TILE = 8
 RIM = 8
-SHAPE = {"c": 2, "x": 4}
+SHAPE = {"c": 2, "x": 4, "yl": 2}
 F32 = jnp.float32
 BF16 = jnp.bfloat16
 CTX = ("z", "c")
-CH = ("x", "y")
+CH = ("x", "yh", "yl")
+DEEP = ("x", "yl")
 VMEM = pl.BlockSpec(memory_space=pltpu.VMEM)
 SMEM = pl.BlockSpec(memory_space=pltpu.SMEM)
 
@@ -114,31 +115,46 @@
 
     lax.fori_loop(0, STRETCH // TILE, eight, 0)
     turned = gated[...].T.astype(BF16)
-    blocks, copies, height, _ = out.shape
-    for b in range(blocks):
-        for copy in range(copies):
-            out[b, copy] = turned[b * height : (b + 1) * height, :]
+    outer, copies, inner_blocks, height, _ = out.shape
+    for b in range(outer):
+        for l in range(inner_blocks):
+            at = (b * inner_blocks + l) * height
+            for copy in range(copies):
+                out[b, copy, l] = turned[at : at + height, :]
 
 
 def project_kernel(gated, weight_at, out, weight, sems):
     parts = out.shape[0]
-    copies = [pltpu.make_async_copy(weight_at.at[:, i], weight.at[i], sems.at[i]) for i in range(parts)]
+    groups, length, height, wide = weight.shape
+    share = parts // groups
+    single = wide // share
+    copies = [
+        pltpu.make_async_copy(
+            weight_at.at[:, i],
+            weight.at[i // share, :, :, pl.ds((i % share) * single, single)],
+            sems.at[i],
+        )
+        for i in range(parts)
+    ]
     for copy in copies:
         copy.start()
-    depth = gated.shape[0] * gated.shape[1]
+    depth = length * height
     left = gated[...].reshape(depth, gated.shape[2])
-    for i in range(parts):
-        copies[i].wait()
-        right = weight[i].reshape(depth, weight.shape[3])
+    for i in range(groups):
+        for copy in copies[i * share : (i + 1) * share]:
+            copy.wait()
+        right = weight[i].reshape(depth, wide)
         total = lax.dot_general(left, right, (((0,), (0,)), ((), ())), preferred_element_type=F32)
-        out[i] = total.astype(BF16)
+        for j in range(share):
+            out[i * share + j] = total[:, j * single : (j + 1) * single].astype(BF16)
 
 
 def mixed_of(features, short_weight, rates, residues, skip, out_weight):
     streams, rows, chans = features.shape
     modes = rates.shape[1]
     length = lax.axis_size(CTX)
-    zs, xs, ys = lax.axis_size("z"), lax.axis_size("x"), lax.axis_size("y")
+    zs, xs, yh, yl = (lax.axis_size(name) for name in ("z", "x", "yh", "yl"))
+    splits = xs * yl
     place = jnp.stack([lax.axis_index("z"), lax.axis_index("c")]).astype(jnp.int32)
     decay_rate = rates.T
     mode_gain = residues.T
@@ -146,10 +162,11 @@
 
     deep, wide = out_weight.shape
     owned = deep // chans
-    piece = chans // xs
+    piece = chans // splits
     height = owned * piece
-    sliced = out_weight.reshape(owned, xs, piece, wide).transpose(1, 0, 2, 3).reshape(xs, height, wide)
-    sliced = lax.all_to_all(sliced, "x", split_axis=0, concat_axis=0, tiled=True)
+    sliced = out_weight.reshape(owned, splits, piece, wide).transpose(1, 0, 2, 3)
+    sliced = sliced.reshape(splits, height, wide)
+    sliced = lax.all_to_all(sliced, DEEP, split_axis=0, concat_axis=0, tiled=True)
     weights = lax.all_gather(sliced, CTX, axis=0, tiled=False)
 
     rim = lax.ppermute(features[:, rows - RIM :, :], CTX, [(i, i + 1) for i in range(length - 1)])
@@ -188,7 +205,7 @@
     )
     spread = pl.pallas_call(
         join_kernel,
-        out_shape=shape((xs, ys, piece, rows), BF16),
+        out_shape=shape((xs, yh, yl, piece, rows), BF16),
         in_specs=[SMEM] + [VMEM] * 7,
         out_specs=VMEM,
         scratch_shapes=[
@@ -201,31 +218,35 @@
         name="join",
     )(place, everyone, pair, before, decays, slope, inner, query)
     gathered = lax.all_to_all(
-        spread.reshape(xs * ys, piece, rows), CH, split_axis=0, concat_axis=0, tiled=True
-    )
-    weights = pltpu.with_memory_space_constraint(weights.reshape(length, xs, height, wide), pltpu.HBM)
+        spread.reshape(xs * yh * yl, piece, rows), CH, split_axis=0, concat_axis=0, tiled=True
+    )
+    weights = pltpu.with_memory_space_constraint(weights.reshape(length, splits, height, wide), pltpu.HBM)
     partial = pl.pallas_call(
         project_kernel,
-        out_shape=shape((xs, rows, wide), BF16),
+        out_shape=shape((splits, rows, wide), BF16),
         in_specs=[VMEM, pl.BlockSpec(memory_space=pl.ANY)],
         out_specs=VMEM,
-        scratch_shapes=[pltpu.VMEM((xs, length, height, wide), BF16), pltpu.SemaphoreType.DMA((xs,))],
+        scratch_shapes=[
+            pltpu.VMEM((splits // 2, length, height, 2 * wide), BF16),
+            pltpu.SemaphoreType.DMA((splits,)),
+        ],
         cost_estimate=pl.CostEstimate(
-            flops=2 * rows * xs * ys * piece * wide * xs, bytes_accessed=6_000_000, transcendentals=0
+            flops=2 * rows * length * height * wide * splits, bytes_accessed=6_000_000, transcendentals=0
         ),
         compiler_params=pltpu.CompilerParams(vmem_limit_bytes=32 << 20),
         name="project",
     )(gathered, weights)
-    shares = lax.all_to_all(partial, "x", split_axis=0, concat_axis=0, tiled=True)
+    shares = lax.all_to_all(partial, DEEP, split_axis=0, concat_axis=0, tiled=True)
     total = shares[0].astype(F32)
-    for i in range(1, xs):
+    for i in range(1, splits):
         total = total + shares[i].astype(F32)
     return total.astype(BF16)
 
 
 def solution(mesh):
-    cores, xs = SHAPE["c"], SHAPE["x"]
-    fine = Mesh(mesh.devices.reshape(-1, cores, xs, mesh.shape["ch"] // xs), ("z", "c", "x", "y"))
+    cores, xs, yl = SHAPE["c"], SHAPE["x"], SHAPE["yl"]
+    yh = mesh.shape["ch"] // (xs * yl)
+    fine = Mesh(mesh.devices.reshape(-1, cores, xs, yh, yl), CTX + CH)
     return jax.shard_map(
         mixed_of,
         mesh=fine,

time: 111 us -> 106 us (0.955)
  blocking collectives: 84.5 us -> 80.4 us
    all_gather x1, blocking collectives: 4.58 us -> 1.83 us  [mixed_of(): pair = lax.all_gather(totals, 'c', axis=0, tiled=False)]
where the time goes in v6:
time: 106 us
  blocking collectives  80.4 us (76%)
  between operations  13.4 us (13%)
  Pallas kernels  7.12 us (7%)
  local copies, waits for them, and re-layouts  1.7 us (2%)
  starting transfers between devices  1.28 us (1%)
    all_to_all x1, blocking collectives, mixed_of(): lax.all_to_all(spread.reshape(xs * yh * yl, piece, rows), CH, split_axis=...  24.4 us
    all_to_all x1, blocking collectives, mixed_of(): lax.all_to_all(jnp.broadcast_to(chip[None], (zs, modes, chans)), 'z', spl...  22.2 us
    all_to_all x1, blocking collectives, mixed_of(): lax.all_to_all(partial, DEEP, split_axis=0, concat_axis=0, tiled=True)  17 us
    all_to_all x1, blocking collectives, mixed_of(): lax.all_to_all(sliced, DEEP, split_axis=0, concat_axis=0, tiled=True)  15 us
    pallas_call x1, Pallas kernels, mixed_of(): pl.pallas_call(project_kernel, out_shape=shape((splits, rows, wide), BF16...  3.06 us
    pallas_call x1, Pallas kernels, mixed_of(): pl.pallas_call(local_kernel, out_shape=shapes, in_specs=[pl.BlockSpec(mem...  2.94 us
  transfers between devices with their start and end apart: 2, of which 1 were waited for; matrix products, arithmetic and copies ran while one was open for 1% of the time, Pallas kernels for 4%

profile of v6, /device:TPU:8, one launch (start us, length us, event | category | flops | bytes accessed | tf_op | source)
XLA Modules:
  0.0 105.5 jit_solution(621778125279800841)
XLA Ops:
  6.5 0.0 all-gather.4.cloned.1.call-start
  6.5 1.0 copy.8
  7.5 15.0 %all_to_all.20 = bf16[8,64,256]{2,1,0:T(8,128)(2,1)} all-to-all(bf16[8,64,256]{2,1,0:T(8,128)(2,1)S(1)} %bitcast.31), channel_id=1, replica_groups=mesh['z'=8,'c'=2,'x'=4,'yh'=4,'yl'=2] {'x','yl'}, dimensions={0} | all-to-all | bytes 524288 | tf_op jit(solution)/shard_map/all_to_all | solution.py:169
  22.5 0.0 all-gather.4.cloned.1.call-update
  22.5 0.7 slice.36
  23.2 1.3 %collective-permute-start = (bf16[3,8,256]{2,1,0:T(8,128)(2,1)S(1)}, bf16[3,8,256]{2,1,0:T(8,128)(2,1)S(1)}, u32[]{:S(2)}, u32[]{:S(2)}) collective-permute-start(bf16[3,8,256]{2,1,0:T(8,128)(2,1)S(1)} %slice.36), channel_id=1, source_target_pairs={{0,32},{32,64},{64,96},{96,128},{128,160},{160,192},{192,224},{224... | collective-permute-start | bytes 36872 | tf_op jit(solution)/shard_map/ppermute | solution.py:172
  24.5 0.1 pad_add_fusion.place
  24.6 0.7 collective-permute-done.rim
  25.3 2.9 %local.1 = (bf16[256,256]{1,0:T(8,128)(2,1)S(1)}, f32[256,256]{1,0:T(8,128)S(1)}, f32[4,16,256]{2,1,0:T(8,128)S(1)}, f32[6,16,256]{2,1,0:T(8,128)S(1)}, f32[16,8...) custom-call(bf16[3,256,256]{2,1,0:T(8,128)(2,1)} %features_at.1, f32[3,7,256]{2,1,0:T(8,128)} %taps_at.1, f32[16,256]{1,0:T(8,128)} %bitcast.33, ...), custom_call_target="tpu_custom_call" | custom-call | flops 8000000 | bytes 2000000 | tf_op jit(solution)/shard_map/local/pallas_call | solution.py:186
  28.3 1.8 %all-gather = f32[32,256]{1,0:T(8,128)S(1)} all-gather(f32[16,256]{1,0:T(8,128)S(1)} %get-tuple-element.16), channel_id=2, replica_groups=mesh['z'=8,'c'=2,'x'=4,'yh'=4,'yl'=2] {'c'}, dimensions={0}, use_global_device_ids=true | all-gather | bytes 49152 | tf_op jit(solution)/shard_map/all_gather | solution.py:201
  30.1 22.2 %all_to_all.21.everyone = f32[8,16,256]{2,1,0:T(8,128)S(1)} all-to-all(f32[8,16,256]{2,1,0:T(8,128)S(1)} %broadcast_in_dim.13), channel_id=1, replica_groups=mesh['z'=8,'c'=2,'x'=4,'yh'=4,'yl'=2] {'z'}, dimensions={0} | all-to-all | bytes 262144 | tf_op jit(solution)/shard_map/all_to_all | solution.py:203
  52.3 1.1 %join.1 = bf16[4,4,2,32,256]{4,3,2,1,0:T(8,128)(2,1)S(1)} custom-call(s32[2]{0:T(128)S(1)} %pad_add_fusion.place, f32[8,16,256]{2,1,0:T(8,128)S(1)} %all_to_all.21.everyone, f32[2,16,256]{2,1,0:T(8,128)S(1)} %bitcast.29, f32[4,16,256]{2,1,0:T(8,128)S(1)} %get-tuple-element.17.before, f32[6,16,256]{2,1,0:T(8,128)S(1)} %get-tuple-element.15.decays, ...), custom_call_target="tpu_custom_call" | custom-call | flops 4000000 | bytes 4000000 | tf_op jit(solution)/shard_map/join/pallas_call | solution.py:206
  53.4 24.4 %all_to_all.22.gated = bf16[32,32,256]{2,1,0:T(8,128)(2,1)S(1)} all-to-all(bf16[32,32,256]{2,1,0:T(8,128)(2,1)S(1)} %bitcast.28), channel_id=1, replica_groups=mesh['z'=8,'c'=2,'x'=4,'yh'=4,'yl'=2] {'x','yh','yl'}, dimensions={0} | all-to-all | bytes 1048576 | tf_op jit(solution)/shard_map/all_to_all | solution.py:220
  77.8 0.0 all-gather.4.cloned.1.call-done
  77.8 3.1 %project.1 = bf16[8,256,256]{2,1,0:T(8,128)(2,1)S(1)} custom-call(bf16[32,32,256]{2,1,0:T(8,128)(2,1)S(1)} %all_to_all.22.gated, bf16[16,8,64,256]{3,2,1,0:T(8,128)(2,1)} %bitcast.30), custom_call_target="tpu_custom_call" | custom-call | flops 1073741824 | bytes 6000000 | tf_op jit(solution)/shard_map/project/pallas_call | solution.py:224
  80.9 17.0 %all_to_all.23 = bf16[8,256,256]{2,1,0:T(8,128)(2,1)S(1)} all-to-all(bf16[8,256,256]{2,1,0:T(8,128)(2,1)S(1)} %project.1), channel_id=1, replica_groups=mesh['z'=8,'c'=2,'x'=4,'yh'=4,'yl'=2] {'x','yl'}, dimensions={0} | all-to-all | bytes 2097152 | tf_op jit(solution)/shard_map/all_to_all | solution.py:239
  97.9 0.8 fusion
  (2 shorter events, 0.0 us)
Async XLA Ops:
  6.5 71.3 %all-gather.4.cloned.1.call-start = ((), (), s32[]{:S(2)}) async-start(), calls=%async_computation.4 | async-start | bytes 4456448 | tf_op jit(solution)/shard_map/all_gather | solution.py:170
  23.2 2.1 %collective-permute-start = (bf16[3,8,256]{2,1,0:T(8,128)(2,1)S(1)}, bf16[3,8,256]{2,1,0:T(8,128)(2,1)S(1)}, u32[]{:S(2)}, u32[]{:S(2)}) collective-permute-start(bf16[3,8,256]{2,1,0:T(8,128)(2,1)S(1)} %slice.36), channel_id=1, source_target_pairs={{0,32},{32,64},{64,96},{96,128},{128,160},{160,192},{192,224},{224... | collective-permute-start | bytes 36872 | tf_op jit(solution)/shard_map/ppermute | solution.py:172
Sparse Core Ops, SparseCore 0:
  22.6 46.3 all-gather.3

commit v7 on v6

--- a/solution.py
+++ b/solution.py
@@ -15,7 +15,7 @@
 BF16 = jnp.bfloat16
 CTX = ("z", "c")
 CH = ("x", "yh", "yl")
-DEEP = ("x", "yl")
+DEEP = ("yl", "x")
 VMEM = pl.BlockSpec(memory_space=pltpu.VMEM)
 SMEM = pl.BlockSpec(memory_space=pltpu.SMEM)
 
@@ -115,12 +115,10 @@
 
     lax.fori_loop(0, STRETCH // TILE, eight, 0)
     turned = gated[...].T.astype(BF16)
-    outer, copies, inner_blocks, height, _ = out.shape
-    for b in range(outer):
-        for l in range(inner_blocks):
-            at = (b * inner_blocks + l) * height
-            for copy in range(copies):
-                out[b, copy, l] = turned[at : at + height, :]
+    blocks, copies, height, _ = out.shape
+    for b in range(blocks):
+        for copy in range(copies):
+            out[b, copy] = turned[b * height : (b + 1) * height, :]
 
 
 def project_kernel(gated, weight_at, out, weight, sems):
@@ -161,11 +159,9 @@
     shape = jax.ShapeDtypeStruct
 
     deep, wide = out_weight.shape
-    owned = deep // chans
-    piece = chans // splits
-    height = owned * piece
-    sliced = out_weight.reshape(owned, splits, piece, wide).transpose(1, 0, 2, 3)
-    sliced = sliced.reshape(splits, height, wide)
+    piece = chans // xs
+    height = deep // splits
+    sliced = out_weight.reshape(splits, height, wide)
     sliced = lax.all_to_all(sliced, DEEP, split_axis=0, concat_axis=0, tiled=True)
     weights = lax.all_gather(sliced, CTX, axis=0, tiled=False)
 
@@ -205,7 +201,7 @@
     )
     spread = pl.pallas_call(
         join_kernel,
-        out_shape=shape((xs, yh, yl, piece, rows), BF16),
+        out_shape=shape((xs, yh, piece, rows), BF16),
         in_specs=[SMEM] + [VMEM] * 7,
         out_specs=VMEM,
         scratch_shapes=[
@@ -218,7 +214,7 @@
         name="join",
     )(place, everyone, pair, before, decays, slope, inner, query)
     gathered = lax.all_to_all(
-        spread.reshape(xs * yh * yl, piece, rows), CH, split_axis=0, concat_axis=0, tiled=True
+        spread.reshape(xs * yh, piece, rows), ("x", "yh"), split_axis=0, concat_axis=0, tiled=True
     )
     weights = pltpu.with_memory_space_constraint(weights.reshape(length, splits, height, wide), pltpu.HBM)
     partial = pl.pallas_call(

time: 106 us -> 105 us (level)
  no operation moved by 1% of the time
where the time goes in v7:
time: 105 us
  blocking collectives  80.6 us (77%)
  between operations  13.4 us (13%)
  Pallas kernels  7.12 us (7%)
  starting transfers between devices  1.28 us (1%)
    all_to_all x1, blocking collectives, mixed_of(): lax.all_to_all(spread.reshape(xs * yh, piece, rows), ('x', 'yh'), split_a...  24.9 us
    all_to_all x1, blocking collectives, mixed_of(): lax.all_to_all(jnp.broadcast_to(chip[None], (zs, modes, chans)), 'z', spl...  21.3 us
    all_to_all x1, blocking collectives, mixed_of(): lax.all_to_all(partial, DEEP, split_axis=0, concat_axis=0, tiled=True)  16.9 us
    all_to_all x1, blocking collectives, mixed_of(): lax.all_to_all(sliced, DEEP, split_axis=0, concat_axis=0, tiled=True)  15.7 us
    pallas_call x1, Pallas kernels, mixed_of(): pl.pallas_call(project_kernel, out_shape=shape((splits, rows, wide), BF16...  3.06 us
    pallas_call x1, Pallas kernels, mixed_of(): pl.pallas_call(local_kernel, out_shape=shapes, in_specs=[pl.BlockSpec(mem...  2.94 us
  transfers between devices with their start and end apart: 2, of which 1 were waited for; matrix products, arithmetic and copies ran while one was open for 1% of the time, Pallas kernels for 4%

profile of v7, /device:TPU:8, one launch (start us, length us, event | category | flops | bytes accessed | tf_op | source)
XLA Modules:
  0.0 104.8 jit_solution(17378363701096904613)
XLA Ops:
  6.5 0.0 all-gather.4.cloned.1.call-start
  6.5 15.7 %all_to_all.20 = bf16[8,64,256]{2,1,0:T(8,128)(2,1)} all-to-all(bf16[8,64,256]{2,1,0:T(8,128)(2,1)} %bitcast.28), channel_id=1, replica_groups=mesh['z'=8,'c'=2,'x'=4,'yh'=4,'yl'=2] {'yl','x'}, dimensions={0} | all-to-all | bytes 524288 | tf_op jit(solution)/shard_map/all_to_all | solution.py:165
  22.2 0.0 all-gather.4.cloned.1.call-update
  22.2 0.7 slice.36
  22.9 1.3 %collective-permute-start = (bf16[3,8,256]{2,1,0:T(8,128)(2,1)S(1)}, bf16[3,8,256]{2,1,0:T(8,128)(2,1)S(1)}, u32[]{:S(2)}, u32[]{:S(2)}) collective-permute-start(bf16[3,8,256]{2,1,0:T(8,128)(2,1)S(1)} %slice.36), channel_id=1, source_target_pairs={{0,32},{32,64},{64,96},{96,128},{128,160},{160,192},{192,224},{224... | collective-permute-start | bytes 36872 | tf_op jit(solution)/shard_map/ppermute | solution.py:168
  24.2 0.1 pad_add_fusion.place
  24.3 0.7 collective-permute-done.rim
  25.0 2.9 %local.1 = (bf16[256,256]{1,0:T(8,128)(2,1)S(1)}, f32[256,256]{1,0:T(8,128)S(1)}, f32[4,16,256]{2,1,0:T(8,128)S(1)}, f32[6,16,256]{2,1,0:T(8,128)S(1)}, f32[16,8...) custom-call(bf16[3,256,256]{2,1,0:T(8,128)(2,1)} %features_at.1, f32[3,7,256]{2,1,0:T(8,128)} %taps_at.1, f32[16,256]{1,0:T(8,128)} %bitcast.29, ...), custom_call_target="tpu_custom_call" | custom-call | flops 8000000 | bytes 2000000 | tf_op jit(solution)/shard_map/local/pallas_call | solution.py:182
  28.0 1.8 %all-gather = f32[32,256]{1,0:T(8,128)S(1)} all-gather(f32[16,256]{1,0:T(8,128)S(1)} %get-tuple-element.16), channel_id=2, replica_groups=mesh['z'=8,'c'=2,'x'=4,'yh'=4,'yl'=2] {'c'}, dimensions={0}, use_global_device_ids=true | all-gather | bytes 49152 | tf_op jit(solution)/shard_map/all_gather | solution.py:197
  29.8 21.3 %all_to_all.21.everyone = f32[8,16,256]{2,1,0:T(8,128)S(1)} all-to-all(f32[8,16,256]{2,1,0:T(8,128)S(1)} %broadcast_in_dim.13), channel_id=1, replica_groups=mesh['z'=8,'c'=2,'x'=4,'yh'=4,'yl'=2] {'z'}, dimensions={0} | all-to-all | bytes 262144 | tf_op jit(solution)/shard_map/all_to_all | solution.py:199
  51.2 1.1 %join.1 = bf16[4,4,64,256]{3,2,1,0:T(8,128)(2,1)S(1)} custom-call(s32[2]{0:T(128)S(1)} %pad_add_fusion.place, f32[8,16,256]{2,1,0:T(8,128)S(1)} %all_to_all.21.everyone, f32[2,16,256]{2,1,0:T(8,128)S(1)} %bitcast.26, f32[4,16,256]{2,1,0:T(8,128)S(1)} %get-tuple-element.17.before, f32[6,16,256]{2,1,0:T(8,128)S(1)} %get-tuple-element.15.decays, ...), custom_call_target="tpu_custom_call" | custom-call | flops 4000000 | bytes 4000000 | tf_op jit(solution)/shard_map/join/pallas_call | solution.py:202
  52.3 24.9 %all_to_all.22.gated = bf16[16,64,256]{2,1,0:T(8,128)(2,1)S(1)} all-to-all(bf16[16,64,256]{2,1,0:T(8,128)(2,1)S(1)} %bitcast.25), channel_id=1, replica_groups=mesh['z'=8,'c'=2,'x'=4,'yh'=4,'yl'=2] {'x','yh'}, dimensions={0} | all-to-all | bytes 1048576 | tf_op jit(solution)/shard_map/all_to_all | solution.py:216
  77.2 0.0 all-gather.4.cloned.1.call-done
  77.2 3.1 %project.1 = bf16[8,256,256]{2,1,0:T(8,128)(2,1)S(1)} custom-call(bf16[16,64,256]{2,1,0:T(8,128)(2,1)S(1)} %all_to_all.22.gated, bf16[16,8,64,256]{3,2,1,0:T(8,128)(2,1)} %bitcast.27), custom_call_target="tpu_custom_call" | custom-call | flops 1073741824 | bytes 6000000 | tf_op jit(solution)/shard_map/project/pallas_call | solution.py:220
  80.3 16.9 %all_to_all.23 = bf16[8,256,256]{2,1,0:T(8,128)(2,1)S(1)} all-to-all(bf16[8,256,256]{2,1,0:T(8,128)(2,1)S(1)} %project.1), channel_id=1, replica_groups=mesh['z'=8,'c'=2,'x'=4,'yh'=4,'yl'=2] {'yl','x'}, dimensions={0} | all-to-all | bytes 2097152 | tf_op jit(solution)/shard_map/all_to_all | solution.py:235
  97.2 0.8 fusion
  (2 shorter events, 0.0 us)
Async XLA Ops:
  6.5 70.7 %all-gather.4.cloned.1.call-start = ((), (), s32[]{:S(2)}) async-start(), calls=%async_computation.4 | async-start | bytes 4456448 | tf_op jit(solution)/shard_map/all_gather | solution.py:166
  22.9 2.1 %collective-permute-start = (bf16[3,8,256]{2,1,0:T(8,128)(2,1)S(1)}, bf16[3,8,256]{2,1,0:T(8,128)(2,1)S(1)}, u32[]{:S(2)}, u32[]{:S(2)}) collective-permute-start(bf16[3,8,256]{2,1,0:T(8,128)(2,1)S(1)} %slice.36), channel_id=1, source_target_pairs={{0,32},{32,64},{64,96},{96,128},{128,160},{160,192},{192,224},{224... | collective-permute-start | bytes 36872 | tf_op jit(solution)/shard_map/ppermute | solution.py:168
Sparse Core Ops, SparseCore 0:
  22.3 45.6 all-gather.3

commit v8 on v7

--- a/solution.py
+++ b/solution.py
@@ -163,10 +163,11 @@
     height = deep // splits
     sliced = out_weight.reshape(splits, height, wide)
     sliced = lax.all_to_all(sliced, DEEP, split_axis=0, concat_axis=0, tiled=True)
+
+    edge = features[:, rows - RIM :, :]
+    rim = lax.ppermute(edge, CTX, [(i, i + 1) for i in range(length - 1)])
+    rim, place, sliced = lax.optimization_barrier((rim, place, sliced))
     weights = lax.all_gather(sliced, CTX, axis=0, tiled=False)
-
-    rim = lax.ppermute(features[:, rows - RIM :, :], CTX, [(i, i + 1) for i in range(length - 1)])
-    rim, place = lax.optimization_barrier((rim, place))
 
     stretches = rows // STRETCH
     shapes = (

time: 105 us -> 102 us (0.971)
  the two profiles are of different devices: /device:TPU:8 before, /device:TPU:16 now
where the time goes in v8:
time: 102 us; the launch traced here: 101 us
  blocking collectives  65.1 us (64%)
  between operations  13.4 us (13%)
  Pallas kernels  7.1 us (7%)
  starting transfers between devices  6.8 us (7%)
  waiting for transfers between devices  6.41 us (6%)
  local copies, waits for them, and re-layouts  1.44 us (1%)
    all_to_all x1, blocking collectives, mixed_of(): lax.all_to_all(spread.reshape(xs * yh, piece, rows), ('x', 'yh'), split_a...  22.6 us
    all_to_all x1, blocking collectives, mixed_of(): lax.all_to_all(partial, DEEP, split_axis=0, concat_axis=0, tiled=True)  21 us
    all_to_all x1, blocking collectives, mixed_of(): lax.all_to_all(jnp.broadcast_to(chip[None], (zs, modes, chans)), 'z', spl...  19.6 us
    all_to_all x1, starting transfers between devices, mixed_of(): lax.all_to_all(sliced, DEEP, split_axis=0, concat_axis=0, tiled=True)  5.31 us
    all_to_all x1, waiting for transfers between devices, mixed_of(): lax.all_to_all(sliced, DEEP, split_axis=0, concat_axis=0, tiled=True)  4.19 us
    pallas_call x1, Pallas kernels, mixed_of(): pl.pallas_call(project_kernel, out_shape=shape((splits, rows, wide), BF16...  3.06 us
    pallas_call x1, Pallas kernels, mixed_of(): pl.pallas_call(local_kernel, out_shape=shapes, in_specs=[pl.BlockSpec(mem...  2.94 us
  transfers between devices with their start and end apart: 3, of which 3 were waited for; matrix products, arithmetic and copies ran while one was open for 1% of the time, Pallas kernels for 4%

profile of v8, /device:TPU:16, one launch (start us, length us, event | category | flops | bytes accessed | tf_op | source)
XLA Modules:
  0.0 101.1 jit_solution(15978176033778102759)
XLA Ops:
  6.5 5.3 %all-to-all-start = ((bf16[8,64,256]{2,1,0:T(8,128)(2,1)}), bf16[8,64,256]{2,1,0:T(8,128)(2,1)S(1)}, u32[]{:S(2)}, u32[]{:S(2)}) async-start(bf16[8,64,256]{2,1,0:T(8,128)(2,1)} %bitcast.28), calls=%async_computation | async-start | bytes 524288 | tf_op jit(solution)/shard_map/all_to_all | solution.py:165
  11.8 0.0 all-gather.4.cloned.1.call-start
  11.9 0.7 slice.36
  12.6 1.4 %collective-permute-start = (bf16[3,8,256]{2,1,0:T(8,128)(2,1)S(1)}, bf16[3,8,256]{2,1,0:T(8,128)(2,1)S(1)}, u32[]{:S(2)}, u32[]{:S(2)}) collective-permute-start(bf16[3,8,256]{2,1,0:T(8,128)(2,1)S(1)} %slice.36), channel_id=1, source_target_pairs={{0,32},{32,64},{64,96},{96,128},{128,160},{160,192},{192,224},{224... | collective-permute-start | bytes 36872 | tf_op jit(solution)/shard_map/ppermute | solution.py:168
  14.1 0.1 pad_add_fusion.place
  14.2 0.7 collective-permute-done.rim
  14.9 4.2 %all-to-all-done = bf16[8,64,256]{2,1,0:T(8,128)(2,1)S(1)} async-done(((bf16[8,64,256]{2,1,0:T(8,128)(2,1)}), bf16[8,64,256]{2,1,0:T(8,128)(2,1)S(1)}, u32[]{:S(2)}, u32[]{:S(2)}) %all-to-all-start) | async-done | bytes 262176 | tf_op jit(solution)/shard_map/all_to_all | solution.py:165
  19.1 0.0 copy-start
  19.1 0.7 copy-done
  19.8 0.0 all-gather.4.cloned.1.call-update
  19.8 2.9 %local.1 = (bf16[256,256]{1,0:T(8,128)(2,1)S(1)}, f32[256,256]{1,0:T(8,128)S(1)}, f32[4,16,256]{2,1,0:T(8,128)S(1)}, f32[6,16,256]{2,1,0:T(8,128)S(1)}, f32[16,8...) custom-call(bf16[3,256,256]{2,1,0:T(8,128)(2,1)} %features_at.1, f32[3,7,256]{2,1,0:T(8,128)} %taps_at.1, f32[16,256]{1,0:T(8,128)} %bitcast.29, ...), custom_call_target="tpu_custom_call" | custom-call | flops 8000000 | bytes 2000000 | tf_op jit(solution)/shard_map/local/pallas_call | solution.py:183
  22.8 1.8 %all-gather = f32[32,256]{1,0:T(8,128)S(1)} all-gather(f32[16,256]{1,0:T(8,128)S(1)} %get-tuple-element.17), channel_id=2, replica_groups=mesh['z'=8,'c'=2,'x'=4,'yh'=4,'yl'=2] {'c'}, dimensions={0}, use_global_device_ids=true | all-gather | bytes 49152 | tf_op jit(solution)/shard_map/all_gather | solution.py:198
  24.6 19.6 %all_to_all.20.everyone = f32[8,16,256]{2,1,0:T(8,128)S(1)} all-to-all(f32[8,16,256]{2,1,0:T(8,128)S(1)} %broadcast_in_dim.13), channel_id=1, replica_groups=mesh['z'=8,'c'=2,'x'=4,'yh'=4,'yl'=2] {'z'}, dimensions={0} | all-to-all | bytes 262144 | tf_op jit(solution)/shard_map/all_to_all | solution.py:200
  44.2 1.1 %join.1 = bf16[4,4,64,256]{3,2,1,0:T(8,128)(2,1)S(1)} custom-call(s32[2]{0:T(128)S(1)} %pad_add_fusion.place, f32[8,16,256]{2,1,0:T(8,128)S(1)} %all_to_all.20.everyone, f32[2,16,256]{2,1,0:T(8,128)S(1)} %bitcast.26, f32[4,16,256]{2,1,0:T(8,128)S(1)} %get-tuple-element.18.before, f32[6,16,256]{2,1,0:T(8,128)S(1)} %get-tuple-element.16.decays, ...), custom_call_target="tpu_custom_call" | custom-call | flops 4000000 | bytes 4000000 | tf_op jit(solution)/shard_map/join/pallas_call | solution.py:203
  45.3 22.6 %all_to_all.21.gated = bf16[16,64,256]{2,1,0:T(8,128)(2,1)S(1)} all-to-all(bf16[16,64,256]{2,1,0:T(8,128)(2,1)S(1)} %bitcast.25), channel_id=1, replica_groups=mesh['z'=8,'c'=2,'x'=4,'yh'=4,'yl'=2] {'x','yh'}, dimensions={0} | all-to-all | bytes 1048576 | tf_op jit(solution)/shard_map/all_to_all | solution.py:217
  67.9 1.5 %all-gather.4.cloned.1.call-done = bf16[128,64,256]{2,1,0:T(8,128)(2,1)} async-done(((bf16[8,64,256]{2,1,0:T(8,128)(2,1)}), bf16[128,64,256]{2,1,0:T(8,128)(2,1)}) %all-gather.4.cloned.1.call-update) | async-done | bytes 4194320 | tf_op jit(solution)/shard_map/all_gather | solution.py:170
  69.4 3.1 %project.1 = bf16[8,256,256]{2,1,0:T(8,128)(2,1)S(1)} custom-call(bf16[16,64,256]{2,1,0:T(8,128)(2,1)S(1)} %all_to_all.21.gated, bf16[16,8,64,256]{3,2,1,0:T(8,128)(2,1)} %bitcast.27), custom_call_target="tpu_custom_call" | custom-call | flops 1073741824 | bytes 6000000 | tf_op jit(solution)/shard_map/project/pallas_call | solution.py:221
  72.5 21.0 %all_to_all.22 = bf16[8,256,256]{2,1,0:T(8,128)(2,1)S(1)} all-to-all(bf16[8,256,256]{2,1,0:T(8,128)(2,1)S(1)} %project.1), channel_id=1, replica_groups=mesh['z'=8,'c'=2,'x'=4,'yh'=4,'yl'=2] {'yl','x'}, dimensions={0} | all-to-all | bytes 2097152 | tf_op jit(solution)/shard_map/all_to_all | solution.py:236
  93.5 0.8 fusion
  (2 shorter events, 0.0 us)
Async XLA Ops:
  6.5 12.5 %all-to-all-start = ((bf16[8,64,256]{2,1,0:T(8,128)(2,1)}), bf16[8,64,256]{2,1,0:T(8,128)(2,1)S(1)}, u32[]{:S(2)}, u32[]{:S(2)}) async-start(bf16[8,64,256]{2,1,0:T(8,128)(2,1)} %bitcast.28), calls=%async_computation | async-start | bytes 524288 | tf_op jit(solution)/shard_map/all_to_all | solution.py:165
  11.8 57.6 %all-gather.4.cloned.1.call-start = ((), (), s32[]{:S(2)}) async-start(), calls=%async_computation.4 | async-start | bytes 4456448 | tf_op jit(solution)/shard_map/all_gather | solution.py:170
  12.6 2.3 %collective-permute-start = (bf16[3,8,256]{2,1,0:T(8,128)(2,1)S(1)}, bf16[3,8,256]{2,1,0:T(8,128)(2,1)S(1)}, u32[]{:S(2)}, u32[]{:S(2)}) collective-permute-start(bf16[3,8,256]{2,1,0:T(8,128)(2,1)S(1)} %slice.36), channel_id=1, source_target_pairs={{0,32},{32,64},{64,96},{96,128},{128,160},{160,192},{192,224},{224... | collective-permute-start | bytes 36872 | tf_op jit(solution)/shard_map/ppermute | solution.py:168
  19.1 0.7 copy-start
Sparse Core Ops, SparseCore 0:
  19.9 49.4 all-gather.3

commit v9 on v8

--- a/solution.py
+++ b/solution.py
@@ -126,20 +126,23 @@
     groups, length, height, wide = weight.shape
     share = parts // groups
     single = wide // share
+    cuts = 4
+    run = length // cuts
     copies = [
         pltpu.make_async_copy(
-            weight_at.at[:, i],
-            weight.at[i // share, :, :, pl.ds((i % share) * single, single)],
-            sems.at[i],
+            weight_at.at[pl.ds(k * run, run), i],
+            weight.at[i // share, pl.ds(k * run, run), :, pl.ds((i % share) * single, single)],
+            sems.at[i, k],
         )
         for i in range(parts)
+        for k in range(cuts)
     ]
     for copy in copies:
         copy.start()
     depth = length * height
     left = gated[...].reshape(depth, gated.shape[2])
     for i in range(groups):
-        for copy in copies[i * share : (i + 1) * share]:
+        for copy in copies[i * share * cuts : (i + 1) * share * cuts]:
             copy.wait()
         right = weight[i].reshape(depth, wide)
         total = lax.dot_general(left, right, (((0,), (0,)), ((), ())), preferred_element_type=F32)
@@ -225,7 +228,7 @@
         out_specs=VMEM,
         scratch_shapes=[
             pltpu.VMEM((splits // 2, length, height, 2 * wide), BF16),
-            pltpu.SemaphoreType.DMA((splits,)),
+            pltpu.SemaphoreType.DMA((splits, 4)),
         ],
         cost_estimate=pl.CostEstimate(
             flops=2 * rows * length * height * wide * splits, bytes_accessed=6_000_000, transcendentals=0

time: 102 us -> 102 us (level)
  no operation moved by 1% of the time
where the time goes in v9:
time: 102 us; the launch traced here: 101 us
  blocking collectives  65.1 us (64%)
  between operations  13.4 us (13%)
  Pallas kernels  7.43 us (7%)
  starting transfers between devices  6.8 us (7%)
  waiting for transfers between devices  6.41 us (6%)
  local copies, waits for them, and re-layouts  1.44 us (1%)
    all_to_all x1, blocking collectives, mixed_of(): lax.all_to_all(spread.reshape(xs * yh, piece, rows), ('x', 'yh'), split_a...  22.6 us
    all_to_all x1, blocking collectives, mixed_of(): lax.all_to_all(partial, DEEP, split_axis=0, concat_axis=0, tiled=True)  21 us
    all_to_all x1, blocking collectives, mixed_of(): lax.all_to_all(jnp.broadcast_to(chip[None], (zs, modes, chans)), 'z', spl...  19.6 us
    all_to_all x1, starting transfers between devices, mixed_of(): lax.all_to_all(sliced, DEEP, split_axis=0, concat_axis=0, tiled=True)  5.31 us
    all_to_all x1, waiting for transfers between devices, mixed_of(): lax.all_to_all(sliced, DEEP, split_axis=0, concat_axis=0, tiled=True)  4.19 us
    pallas_call x1, Pallas kernels, mixed_of(): pl.pallas_call(project_kernel, out_shape=shape((splits, rows, wide), BF16...  3.38 us
    pallas_call x1, Pallas kernels, mixed_of(): pl.pallas_call(local_kernel, out_shape=shapes, in_specs=[pl.BlockSpec(mem...  2.94 us
  transfers between devices with their start and end apart: 3, of which 3 were waited for; matrix products, arithmetic and copies ran while one was open for 1% of the time, Pallas kernels for 4%

profile of v9, /device:TPU:16, one launch (start us, length us, event | category | flops | bytes accessed | tf_op | source)
XLA Modules:
  0.0 101.4 jit_solution(14149784433123938860)
XLA Ops:
  6.5 5.3 %all-to-all-start = ((bf16[8,64,256]{2,1,0:T(8,128)(2,1)}), bf16[8,64,256]{2,1,0:T(8,128)(2,1)S(1)}, u32[]{:S(2)}, u32[]{:S(2)}) async-start(bf16[8,64,256]{2,1,0:T(8,128)(2,1)} %bitcast.28), calls=%async_computation | async-start | bytes 524288 | tf_op jit(solution)/shard_map/all_to_all | solution.py:168
  11.8 0.0 all-gather.4.cloned.1.call-start
  11.9 0.7 slice.36
  12.6 1.4 %collective-permute-start = (bf16[3,8,256]{2,1,0:T(8,128)(2,1)S(1)}, bf16[3,8,256]{2,1,0:T(8,128)(2,1)S(1)}, u32[]{:S(2)}, u32[]{:S(2)}) collective-permute-start(bf16[3,8,256]{2,1,0:T(8,128)(2,1)S(1)} %slice.36), channel_id=1, source_target_pairs={{0,32},{32,64},{64,96},{96,128},{128,160},{160,192},{192,224},{224... | collective-permute-start | bytes 36872 | tf_op jit(solution)/shard_map/ppermute | solution.py:171
  14.1 0.1 pad_add_fusion.place
  14.2 0.7 collective-permute-done.rim
  14.9 4.2 %all-to-all-done = bf16[8,64,256]{2,1,0:T(8,128)(2,1)S(1)} async-done(((bf16[8,64,256]{2,1,0:T(8,128)(2,1)}), bf16[8,64,256]{2,1,0:T(8,128)(2,1)S(1)}, u32[]{:S(2)}, u32[]{:S(2)}) %all-to-all-start) | async-done | bytes 262176 | tf_op jit(solution)/shard_map/all_to_all | solution.py:168
  19.1 0.0 copy-start
  19.1 0.7 copy-done
  19.8 0.0 all-gather.4.cloned.1.call-update
  19.8 2.9 %local.1 = (bf16[256,256]{1,0:T(8,128)(2,1)S(1)}, f32[256,256]{1,0:T(8,128)S(1)}, f32[4,16,256]{2,1,0:T(8,128)S(1)}, f32[6,16,256]{2,1,0:T(8,128)S(1)}, f32[16,8...) custom-call(bf16[3,256,256]{2,1,0:T(8,128)(2,1)} %features_at.1, f32[3,7,256]{2,1,0:T(8,128)} %taps_at.1, f32[16,256]{1,0:T(8,128)} %bitcast.29, ...), custom_call_target="tpu_custom_call" | custom-call | flops 8000000 | bytes 2000000 | tf_op jit(solution)/shard_map/local/pallas_call | solution.py:186
  22.8 1.8 %all-gather = f32[32,256]{1,0:T(8,128)S(1)} all-gather(f32[16,256]{1,0:T(8,128)S(1)} %get-tuple-element.17), channel_id=2, replica_groups=mesh['z'=8,'c'=2,'x'=4,'yh'=4,'yl'=2] {'c'}, dimensions={0}, use_global_device_ids=true | all-gather | bytes 49152 | tf_op jit(solution)/shard_map/all_gather | solution.py:201
  24.6 19.6 %all_to_all.20.everyone = f32[8,16,256]{2,1,0:T(8,128)S(1)} all-to-all(f32[8,16,256]{2,1,0:T(8,128)S(1)} %broadcast_in_dim.13), channel_id=1, replica_groups=mesh['z'=8,'c'=2,'x'=4,'yh'=4,'yl'=2] {'z'}, dimensions={0} | all-to-all | bytes 262144 | tf_op jit(solution)/shard_map/all_to_all | solution.py:203
  44.2 1.1 %join.1 = bf16[4,4,64,256]{3,2,1,0:T(8,128)(2,1)S(1)} custom-call(s32[2]{0:T(128)S(1)} %pad_add_fusion.place, f32[8,16,256]{2,1,0:T(8,128)S(1)} %all_to_all.20.everyone, f32[2,16,256]{2,1,0:T(8,128)S(1)} %bitcast.26, f32[4,16,256]{2,1,0:T(8,128)S(1)} %get-tuple-element.18.before, f32[6,16,256]{2,1,0:T(8,128)S(1)} %get-tuple-element.16.decays, ...), custom_call_target="tpu_custom_call" | custom-call | flops 4000000 | bytes 4000000 | tf_op jit(solution)/shard_map/join/pallas_call | solution.py:206
  45.3 22.6 %all_to_all.21.gated = bf16[16,64,256]{2,1,0:T(8,128)(2,1)S(1)} all-to-all(bf16[16,64,256]{2,1,0:T(8,128)(2,1)S(1)} %bitcast.25), channel_id=1, replica_groups=mesh['z'=8,'c'=2,'x'=4,'yh'=4,'yl'=2] {'x','yh'}, dimensions={0} | all-to-all | bytes 1048576 | tf_op jit(solution)/shard_map/all_to_all | solution.py:220
  67.9 1.5 %all-gather.4.cloned.1.call-done = bf16[128,64,256]{2,1,0:T(8,128)(2,1)} async-done(((bf16[8,64,256]{2,1,0:T(8,128)(2,1)}), bf16[128,64,256]{2,1,0:T(8,128)(2,1)}) %all-gather.4.cloned.1.call-update) | async-done | bytes 4194320 | tf_op jit(solution)/shard_map/all_gather | solution.py:173
  69.4 3.4 %project.1 = bf16[8,256,256]{2,1,0:T(8,128)(2,1)S(1)} custom-call(bf16[16,64,256]{2,1,0:T(8,128)(2,1)S(1)} %all_to_all.21.gated, bf16[16,8,64,256]{3,2,1,0:T(8,128)(2,1)} %bitcast.27), custom_call_target="tpu_custom_call" | custom-call | flops 1073741824 | bytes 6000000 | tf_op jit(solution)/shard_map/project/pallas_call | solution.py:224
  72.8 21.0 %all_to_all.22 = bf16[8,256,256]{2,1,0:T(8,128)(2,1)S(1)} all-to-all(bf16[8,256,256]{2,1,0:T(8,128)(2,1)S(1)} %project.1), channel_id=1, replica_groups=mesh['z'=8,'c'=2,'x'=4,'yh'=4,'yl'=2] {'yl','x'}, dimensions={0} | all-to-all | bytes 2097152 | tf_op jit(solution)/shard_map/all_to_all | solution.py:239
  93.8 0.8 fusion
  (2 shorter events, 0.0 us)
Async XLA Ops:
  6.5 12.5 %all-to-all-start = ((bf16[8,64,256]{2,1,0:T(8,128)(2,1)}), bf16[8,64,256]{2,1,0:T(8,128)(2,1)S(1)}, u32[]{:S(2)}, u32[]{:S(2)}) async-start(bf16[8,64,256]{2,1,0:T(8,128)(2,1)} %bitcast.28), calls=%async_computation | async-start | bytes 524288 | tf_op jit(solution)/shard_map/all_to_all | solution.py:168
  11.8 57.6 %all-gather.4.cloned.1.call-start = ((), (), s32[]{:S(2)}) async-start(), calls=%async_computation.4 | async-start | bytes 4456448 | tf_op jit(solution)/shard_map/all_gather | solution.py:173
  12.6 2.3 %collective-permute-start = (bf16[3,8,256]{2,1,0:T(8,128)(2,1)S(1)}, bf16[3,8,256]{2,1,0:T(8,128)(2,1)S(1)}, u32[]{:S(2)}, u32[]{:S(2)}) collective-permute-start(bf16[3,8,256]{2,1,0:T(8,128)(2,1)S(1)} %slice.36), channel_id=1, source_target_pairs={{0,32},{32,64},{64,96},{96,128},{128,160},{160,192},{192,224},{224... | collective-permute-start | bytes 36872 | tf_op jit(solution)/shard_map/ppermute | solution.py:171
  19.1 0.7 copy-start
Sparse Core Ops, SparseCore 0:
  19.9 49.4 all-gather.3

commit v10 on v8

--- a/solution.py
+++ b/solution.py
@@ -153,7 +153,6 @@
     length = lax.axis_size(CTX)
     zs, xs, yh, yl = (lax.axis_size(name) for name in ("z", "x", "yh", "yl"))
     splits = xs * yl
-    place = jnp.stack([lax.axis_index("z"), lax.axis_index("c")]).astype(jnp.int32)
     decay_rate = rates.T
     mode_gain = residues.T
     shape = jax.ShapeDtypeStruct
@@ -166,7 +165,9 @@
 
     edge = features[:, rows - RIM :, :]
     rim = lax.ppermute(edge, CTX, [(i, i + 1) for i in range(length - 1)])
-    rim, place, sliced = lax.optimization_barrier((rim, place, sliced))
+    seat, sliced = lax.optimization_barrier(((lax.axis_index("z"), lax.axis_index("c")), sliced))
+    place = jnp.stack(seat).astype(jnp.int32)
+    rim, place = lax.optimization_barrier((rim, place))
     weights = lax.all_gather(sliced, CTX, axis=0, tiled=False)
 
     stretches = rows // STRETCH

time: 102 us -> 106 us (1.039)
  the two profiles are of different devices: /device:TPU:16 before, /device:TPU:8 now
where the time goes in v10:
time: 106 us; the launch traced here: 105 us
  blocking collectives  65.6 us (62%)
  between operations  13.4 us (13%)
  starting transfers between devices  10.4 us (10%)
  Pallas kernels  7.11 us (7%)
  waiting for transfers between devices  6.6 us (6%)
  local copies, waits for them, and re-layouts  1.44 us (1%)
    all_to_all x1, blocking collectives, mixed_of(): lax.all_to_all(spread.reshape(xs * yh, piece, rows), ('x', 'yh'), split_a...  24.9 us
    all_to_all x1, blocking collectives, mixed_of(): lax.all_to_all(jnp.broadcast_to(chip[None], (zs, modes, chans)), 'z', spl...  21.9 us
    all_to_all x1, blocking collectives, mixed_of(): lax.all_to_all(partial, DEEP, split_axis=0, concat_axis=0, tiled=True)  16.9 us
    all_to_all x1, starting transfers between devices, mixed_of(): lax.all_to_all(sliced, DEEP, split_axis=0, concat_axis=0, tiled=True)  9.13 us
    all_to_all x1, waiting for transfers between devices, mixed_of(): lax.all_to_all(sliced, DEEP, split_axis=0, concat_axis=0, tiled=True)  5.84 us
    pallas_call x1, Pallas kernels, mixed_of(): pl.pallas_call(project_kernel, out_shape=shape((splits, rows, wide), BF16...  3.06 us
    pallas_call x1, Pallas kernels, mixed_of(): pl.pallas_call(local_kernel, out_shape=shapes, in_specs=[pl.BlockSpec(mem...  2.93 us
  transfers between devices with their start and end apart: 3, of which 2 were waited for; matrix products, arithmetic and copies ran while one was open for 1% of the time, Pallas kernels for 4%

profile of v10, /device:TPU:8, one launch (start us, length us, event | category | flops | bytes accessed | tf_op | source)
XLA Modules:
  0.0 105.4 jit_solution(11205163679203773220)
XLA Ops:
  6.5 9.1 %all-to-all-start = ((bf16[8,64,256]{2,1,0:T(8,128)(2,1)}), bf16[8,64,256]{2,1,0:T(8,128)(2,1)S(1)}, u32[]{:S(2)}, u32[]{:S(2)}) async-start(bf16[8,64,256]{2,1,0:T(8,128)(2,1)} %bitcast.28), calls=%async_computation | async-start | bytes 524288 | tf_op jit(solution)/shard_map/all_to_all | solution.py:164
  15.7 0.0 all-gather.4.cloned.1.call-start
  15.7 5.8 %all-to-all-done = bf16[8,64,256]{2,1,0:T(8,128)(2,1)S(1)} async-done(((bf16[8,64,256]{2,1,0:T(8,128)(2,1)}), bf16[8,64,256]{2,1,0:T(8,128)(2,1)S(1)}, u32[]{:S(2)}, u32[]{:S(2)}) %all-to-all-start) | async-done | bytes 262176 | tf_op jit(solution)/shard_map/all_to_all | solution.py:164
  21.5 0.0 copy-start
  21.5 0.7 copy-done
  22.2 0.0 all-gather.4.cloned.1.call-update
  22.2 0.7 slice.36
  23.0 1.3 %collective-permute-start = (bf16[3,8,256]{2,1,0:T(8,128)(2,1)S(1)}, bf16[3,8,256]{2,1,0:T(8,128)(2,1)S(1)}, u32[]{:S(2)}, u32[]{:S(2)}) collective-permute-start(bf16[3,8,256]{2,1,0:T(8,128)(2,1)S(1)} %slice.36), channel_id=1, source_target_pairs={{0,32},{32,64},{64,96},{96,128},{128,160},{160,192},{192,224},{224... | collective-permute-start | bytes 36872 | tf_op jit(solution)/shard_map/ppermute | solution.py:167
  24.2 0.1 pad_add_fusion.place
  24.3 0.7 collective-permute-done.rim
  25.1 2.9 %local.1 = (bf16[256,256]{1,0:T(8,128)(2,1)S(1)}, f32[256,256]{1,0:T(8,128)S(1)}, f32[4,16,256]{2,1,0:T(8,128)S(1)}, f32[6,16,256]{2,1,0:T(8,128)S(1)}, f32[16,8...) custom-call(bf16[3,256,256]{2,1,0:T(8,128)(2,1)} %features_at.1, f32[3,7,256]{2,1,0:T(8,128)} %taps_at.1, f32[16,256]{1,0:T(8,128)} %bitcast.29, ...), custom_call_target="tpu_custom_call" | custom-call | flops 8000000 | bytes 2000000 | tf_op jit(solution)/shard_map/local/pallas_call | solution.py:184
  28.0 1.8 %all-gather = f32[32,256]{1,0:T(8,128)S(1)} all-gather(f32[16,256]{1,0:T(8,128)S(1)} %get-tuple-element.21), channel_id=2, replica_groups=mesh['z'=8,'c'=2,'x'=4,'yh'=4,'yl'=2] {'c'}, dimensions={0}, use_global_device_ids=true | all-gather | bytes 49152 | tf_op jit(solution)/shard_map/all_gather | solution.py:199
  29.9 21.9 %all_to_all.20.everyone = f32[8,16,256]{2,1,0:T(8,128)S(1)} all-to-all(f32[8,16,256]{2,1,0:T(8,128)S(1)} %broadcast_in_dim.13), channel_id=1, replica_groups=mesh['z'=8,'c'=2,'x'=4,'yh'=4,'yl'=2] {'z'}, dimensions={0} | all-to-all | bytes 262144 | tf_op jit(solution)/shard_map/all_to_all | solution.py:201
  51.8 1.1 %join.1 = bf16[4,4,64,256]{3,2,1,0:T(8,128)(2,1)S(1)} custom-call(s32[2]{0:T(128)S(1)} %pad_add_fusion.place, f32[8,16,256]{2,1,0:T(8,128)S(1)} %all_to_all.20.everyone, f32[2,16,256]{2,1,0:T(8,128)S(1)} %bitcast.26, f32[4,16,256]{2,1,0:T(8,128)S(1)} %get-tuple-element.22.before, f32[6,16,256]{2,1,0:T(8,128)S(1)} %get-tuple-element.20.decays, ...), custom_call_target="tpu_custom_call" | custom-call | flops 4000000 | bytes 4000000 | tf_op jit(solution)/shard_map/join/pallas_call | solution.py:204
  52.9 24.9 %all_to_all.21.gated = bf16[16,64,256]{2,1,0:T(8,128)(2,1)S(1)} all-to-all(bf16[16,64,256]{2,1,0:T(8,128)(2,1)S(1)} %bitcast.25), channel_id=1, replica_groups=mesh['z'=8,'c'=2,'x'=4,'yh'=4,'yl'=2] {'x','yh'}, dimensions={0} | all-to-all | bytes 1048576 | tf_op jit(solution)/shard_map/all_to_all | solution.py:218
  77.8 0.0 all-gather.4.cloned.1.call-done
  77.8 3.1 %project.1 = bf16[8,256,256]{2,1,0:T(8,128)(2,1)S(1)} custom-call(bf16[16,64,256]{2,1,0:T(8,128)(2,1)S(1)} %all_to_all.21.gated, bf16[16,8,64,256]{3,2,1,0:T(8,128)(2,1)} %bitcast.27), custom_call_target="tpu_custom_call" | custom-call | flops 1073741824 | bytes 6000000 | tf_op jit(solution)/shard_map/project/pallas_call | solution.py:222
  80.9 16.9 %all_to_all.22 = bf16[8,256,256]{2,1,0:T(8,128)(2,1)S(1)} all-to-all(bf16[8,256,256]{2,1,0:T(8,128)(2,1)S(1)} %project.1), channel_id=1, replica_groups=mesh['z'=8,'c'=2,'x'=4,'yh'=4,'yl'=2] {'yl','x'}, dimensions={0} | all-to-all | bytes 2097152 | tf_op jit(solution)/shard_map/all_to_all | solution.py:237
  97.8 0.8 fusion
  (2 shorter events, 0.0 us)
Async XLA Ops:
  6.5 15.0 %all-to-all-start = ((bf16[8,64,256]{2,1,0:T(8,128)(2,1)}), bf16[8,64,256]{2,1,0:T(8,128)(2,1)S(1)}, u32[]{:S(2)}, u32[]{:S(2)}) async-start(bf16[8,64,256]{2,1,0:T(8,128)(2,1)} %bitcast.28), calls=%async_computation | async-start | bytes 524288 | tf_op jit(solution)/shard_map/all_to_all | solution.py:164
  15.7 62.1 %all-gather.4.cloned.1.call-start = ((), (), s32[]{:S(2)}) async-start(), calls=%async_computation.4 | async-start | bytes 4456448 | tf_op jit(solution)/shard_map/all_gather | solution.py:171
  21.5 0.7 copy-start
  23.0 2.1 %collective-permute-start = (bf16[3,8,256]{2,1,0:T(8,128)(2,1)S(1)}, bf16[3,8,256]{2,1,0:T(8,128)(2,1)S(1)}, u32[]{:S(2)}, u32[]{:S(2)}) collective-permute-start(bf16[3,8,256]{2,1,0:T(8,128)(2,1)S(1)} %slice.36), channel_id=1, source_target_pairs={{0,32},{32,64},{64,96},{96,128},{128,160},{160,192},{192,224},{224... | collective-permute-start | bytes 36872 | tf_op jit(solution)/shard_map/ppermute | solution.py:167
Sparse Core Ops, SparseCore 0:
  22.4 46.2 all-gather.3
